TPU v7x, 32 devices: a whole 2x2x4 slice. The times are simulated.
32 devices in a mesh: grp: 2 (over x), wide: 16 (over z, y, core).
Axes of the slice: x: 2, y: 2, z: 4, core: 2. Of those that a mesh axis runs over, the one named last changes fastest.
Arguments:
- hidden_in: bfloat16 [128, 4096], P(('grp', 'wide')), parts along dimension 0, may hold values from -6 to 6
- ffn_gain: float32 [4096], replicated, may hold values from 0.1 to 1.9
- gate_weight: bfloat16 [4096, 14336], P(None, 'wide'), may hold values from -0.09375 to 0.09375
- up_weight: bfloat16 [4096, 14336], P(None, 'wide'), may hold values from -0.09375 to 0.09375
- down_weight: bfloat16 [14336, 4096], P('wide'), may hold values from -0.046875 to 0.046875
- final_gain: float32 [4096], replicated, may hold values from 0.1 to 1.9
- codes: bfloat16 [256, 128, 4096], P(('grp', 'wide')), parts along dimension 0, may hold values from -1 to 1
- scales: float32 [256, 128, 32], P(('grp', 'wide')), parts along dimension 0, may hold values from 0.5 to 5
- counts: int32 [256], P('grp'), parts along dimension 0, may hold values from 1 to 128, 10240 in all
- list_slot: int32 [256], P('grp'), parts along dimension 0, may hold values from 0 to 127, as said below
- probes: int32 [128, 8], P(('grp', 'wide')), parts along dimension 0, may hold values from 0 to 127, as said below
Outputs:
- top_scores: float32 [128, 8], P(('grp', 'wide')), parts along dimension 0
There are 2 independent parts, one for each index of `grp`. A program takes and returns all parts, laid end to end along the dimension named above; an argument that names none is the same for every part. Nothing has to cross between parts.
Inputs may be any that keep to these rules, and one draw needn't show every extreme that they name: Each query names 8 different lists. List l is held by device list_slot[l] // 8; of the 32 probes of one device's queries at most 2 name lists held by one device, and some devices are named 2 times by the queries of every device. `list_slot`: each storage row holds exactly one list. The valid rows of a list are its first counts[l] rows; some list is full.
All inputs are finite; a program needn't handle non-finite values.
Results may differ from a plain program's by a relative error of at most 0.002.
Values may be sent and summed in bfloat16 or wider, within the bound.
No kernel may reach another device: no remote copies, remote signals or barrier semaphores. Data moves between devices by JAX's collectives and lax.ppermute only.
A program may use at most 128 MiB of HBM per device.

v0:
```python
import functools

import jax
import jax.numpy as jnp
from jax import lax
from jax.experimental import pallas as pl
from jax.experimental.pallas import tpu as pltpu
from jax.sharding import PartitionSpec as P


PROBES = 8
K_TOP = 8
BLOCK = 128
LANES = 128
DIGIT = 256
CHUNKS = 2


floor_score = -1e30

VMEM = pltpu.VMEM


def call(kernel, out_shape, args, vmem, cost=None, scratch=()):
    many = isinstance(out_shape, (list, tuple))
    return pl.pallas_call(
        kernel,
        out_shape=out_shape,
        in_specs=[pl.BlockSpec(memory_space=VMEM)] * len(args),
        out_specs=[pl.BlockSpec(memory_space=VMEM)] * len(out_shape)
        if many
        else pl.BlockSpec(memory_space=VMEM),
        scratch_shapes=list(scratch),
        compiler_params=pltpu.CompilerParams(vmem_limit_bytes=vmem),
        cost_estimate=cost,
    )(*args)


def ahead(*arrays):
    total = sum(a.size * a.dtype.itemsize for a in arrays)
    return pl.CostEstimate(flops=1000 * total, bytes_accessed=1 << 20, transcendentals=0)


def products(count):
    return pl.CostEstimate(flops=2 * count, bytes_accessed=1 << 20, transcendentals=0)


def shaped(shape, dtype):
    return jax.ShapeDtypeStruct(shape, dtype)


def norm_kernel(hidden_ref, gain_ref, probes_ref, out_ref, rows_ref, scale_ref, ids_ref, sems):
    copies = [
        pltpu.make_async_copy(source, target, sems.at[index])
        for index, (source, target) in enumerate(
            [(hidden_ref, rows_ref), (gain_ref, scale_ref), (probes_ref, ids_ref)]
        )
    ]
    for copy in copies:
        copy.start()
    for copy in copies:
        copy.wait()
    rows = rows_ref[...].astype(jnp.float32)
    width = rows.shape[1]
    scale = lax.rsqrt(jnp.mean(rows * rows, axis=-1, keepdims=True) + 1e-05)
    out_ref[:, :width] = (rows * scale * scale_ref[...]).astype(jnp.bfloat16)

    q_dev, probes = ids_ref.shape
    pairs = q_dev * probes
    lane = lax.broadcasted_iota(jnp.int32, (q_dev, LANES), 1)
    query = lax.broadcasted_iota(jnp.int32, (q_dev, LANES), 0)
    ids = jnp.zeros((q_dev, LANES), jnp.int32)
    for j in range(probes):
        ids = jnp.where(lane % probes == j, ids_ref[:, j : j + 1], ids)
    ids = jnp.where((lane % pairs) // probes == query, ids, 0)
    ids = jnp.sum(ids, axis=0, keepdims=True)
    digits = jnp.where(lane < pairs, ids // DIGIT, ids % DIGIT)
    digits = jnp.where(lane < 2 * pairs, digits, 0)
    out_ref[:, width:] = digits.astype(jnp.float32).astype(jnp.bfloat16)


def spread_kernel(normed_ref, out_ref):
    half = out_ref.shape[2] - LANES
    for k in range(out_ref.shape[0]):
        core = k % 2
        out_ref[k, :, :half] = normed_ref[:, core * half : (core + 1) * half]
        out_ref[k, :, half:] = normed_ref[:, 2 * half :]


def wanted_kernel(capacity, q_dev, probes, here_ref, slot_ref, after_ref, out_ref):
    devices, _, wide = here_ref.shape
    half = wide - LANES
    lists = slot_ref.shape[1]
    pairs = q_dev * probes
    lists_dev = lists // devices
    me = lax.axis_index("wide")
    tails = here_ref[:, :, half:].astype(jnp.float32)
    tails = jnp.max(tails, axis=1).astype(jnp.int32)
    ids = tails[:, :pairs] * DIGIT + tails[:, pairs : 2 * pairs]
    number = lax.broadcasted_iota(jnp.int32, (1, lists), 1)
    local = jnp.full((devices, pairs), -1, jnp.int32)
    for index in range(lists_dev):
        held = slot_ref[...] == me * lists_dev + index
        mine = jnp.sum(jnp.where(held, number, 0), axis=1, keepdims=True)
        local = jnp.where(ids == mine, index, local)
    pair = lax.broadcasted_iota(jnp.int32, (devices, pairs), 1)
    home = lax.broadcasted_iota(jnp.int32, (devices, 1), 0)
    place = lax.broadcasted_iota(jnp.int32, (devices, LANES), 1)
    side = lax.rem(me, 4) // 2
    before = jnp.full((devices, 1), -1, jnp.int32)
    for rank in range(capacity):
        open_pair = (local >= 0) & (pair > before)
        chosen = jnp.min(jnp.where(open_pair, pair, pairs), axis=1, keepdims=True)
        there = jnp.sum(jnp.where(pair == chosen, local, 0), axis=1, keepdims=True)
        row = jnp.where(
            lax.rem(home, 4) // 2 == side, 0, devices * q_dev // 2
        ) + home // 4 * (2 * q_dev) + lax.rem(home, 2) * q_dev + chosen // probes
        row = jnp.where(chosen < pairs, row, -1)
        out_ref[rank * devices : (rank + 1) * devices, :] = jnp.where(
            place == 0, row, jnp.where(place == 1, there, 0)
        )
        before = chosen


def route_kernel(lists_dev, capacity, probes_ref, slot_ref, count_ref, after_ref, out_ref):
    q_dev, probes = probes_ref.shape
    lists = slot_ref.shape[1]
    pairs = q_dev * probes
    slots = out_ref.shape[0]
    ids = jnp.concatenate(
        [jnp.broadcast_to(probes_ref[q : q + 1, :], (probes, probes)) for q in range(q_dev)], axis=0
    )
    sub = lax.broadcasted_iota(jnp.int32, (pairs, probes), 0)
    lane = lax.broadcasted_iota(jnp.int32, (pairs, probes), 1)
    ids = jnp.sum(jnp.where(sub % probes == lane, ids, 0), axis=1, keepdims=True)
    hit = lax.broadcasted_iota(jnp.int32, (pairs, lists), 1) == ids
    slot = jnp.sum(jnp.where(hit, slot_ref[...], 0), axis=1, keepdims=True)
    valid = jnp.sum(jnp.where(hit, count_ref[...], 0), axis=1, keepdims=True)
    owner = slot // lists_dev
    local = slot % lists_dev
    p_sub = lax.broadcasted_iota(jnp.int32, (pairs, pairs), 0)
    p_lane = lax.broadcasted_iota(jnp.int32, (pairs, pairs), 1)
    diagonal = p_sub == p_lane

    def as_row(column):
        return jnp.sum(jnp.where(diagonal, column, 0), axis=0, keepdims=True)

    owner_row = as_row(owner)
    rank_row = jnp.sum(
        jnp.where((owner == owner_row) & (p_sub < p_lane), 1, 0), axis=0, keepdims=True
    )
    target_row = owner_row * capacity + rank_row
    here = lax.broadcasted_iota(jnp.int32, (slots, pairs), 0) == target_row
    pair_row = lax.broadcasted_iota(jnp.int32, (slots, pairs), 1)

    def of_slot(row):
        return jnp.sum(jnp.where(here, row, 0), axis=1, keepdims=True)

    query = of_slot(pair_row // probes + 1) - 1
    place = lax.broadcasted_iota(jnp.int32, (slots, LANES), 1)
    out = jnp.where(place == 0, query, 0)
    out = jnp.where(place == 1, of_slot(as_row(local)), out)
    out_ref[...] = jnp.where(place == 2, of_slot(as_row(valid)), out)


def my_span(mine, half, start, size):
    core = lax.rem(lax.axis_index("wide"), 2)
    which = core if mine else 1 - core
    return pl.ds(pl.multiple_of(which * half + start, size), size)


def first_kernel(here_ref, gate_ref, up_ref, after_ref, gate_out, up_out, rows_ref):
    rows_ref[...] = here_ref[:, :, : rows_ref.shape[1]].reshape(rows_ref.shape)
    half = rows_ref.shape[1]
    span = my_span(True, half, 0, half)
    gate_out[...] = jnp.dot(rows_ref[...], gate_ref[span, :], preferred_element_type=jnp.float32)
    up_out[...] = jnp.dot(rows_ref[...], up_ref[span, :], preferred_element_type=jnp.float32)


def put_share(act_ref, down_ref, hidden_ref, send_ref, half, start):
    rows, size = act_ref.shape[0], send_ref.shape[1]
    span = my_span(False, half, start, size)
    send_ref[:rows, :] = jnp.dot(
        act_ref[...], down_ref[:, span], preferred_element_type=jnp.float32
    ).astype(jnp.bfloat16)
    residual = hidden_ref[:, span]
    send_ref[rows:, :] = jnp.concatenate([residual, residual], axis=0)


def second_kernel(
    there_ref, gate_part, up_part, gate_ref, up_ref, down_ref, hidden_ref, act_ref, send_ref, rows_ref
):
    half = rows_ref.shape[1]
    rows_ref[...] = there_ref[:, :, :half].reshape(rows_ref.shape)
    span = my_span(False, half, 0, half)
    gate = gate_part[...] + jnp.dot(
        rows_ref[...], gate_ref[span, :], preferred_element_type=jnp.float32
    )
    up = up_part[...] + jnp.dot(
        rows_ref[...], up_ref[span, :], preferred_element_type=jnp.float32
    )
    act_ref[...] = (gate / (1.0 + jnp.exp(-gate)) * up).astype(jnp.bfloat16)
    put_share(act_ref, down_ref, hidden_ref, send_ref, half, 0)


def share_kernel(half, start, act_ref, down_ref, hidden_ref, send_ref):
    put_share(act_ref, down_ref, hidden_ref, send_ref, half, start)


def own_kernel(half, start, act_ref, down_ref, own_ref):
    span = my_span(True, half, start, own_ref.shape[1])
    own_ref[...] = jnp.dot(act_ref[...], down_ref[:, span], preferred_element_type=jnp.float32)


def side_kernel(start, own_ref, came_ref, hidden_ref, keep_ref, send_ref):
    rows, size = own_ref.shape
    q_dev, width = hidden_ref.shape
    half = width // 2
    me = lax.axis_index("wide")
    core, side, plane = lax.rem(me, 2), lax.rem(me, 4) // 2, me // 4
    group = 2 * q_dev
    mine = jnp.where(
        core == 0,
        hidden_ref[:, start : start + size],
        hidden_ref[:, half + start : half + start + size],
    ).astype(jnp.float32)
    other = came_ref[rows : rows + q_dev, :].astype(jnp.float32)
    residual = jnp.where(
        core == 0,
        jnp.concatenate([mine, other], axis=0),
        jnp.concatenate([other, mine], axis=0),
    )
    for z in range(rows // (2 * group)):
        total = []
        for y in range(2):
            span = slice((2 * z + y) * group, (2 * z + y + 1) * group)
            total.append(own_ref[span, :] + came_ref[span, :].astype(jnp.float32))
        kept = jnp.where(side == 0, total[0], total[1])
        sent = jnp.where(side == 0, total[1], total[0])
        span = slice(z * group, (z + 1) * group)
        keep_ref[span, :] = kept + jnp.where(plane == z, residual, jnp.zeros_like(residual))
        send_ref[span, :] = sent.astype(jnp.bfloat16)


def sum_kernel(keep_ref, came_ref, total_ref, send_ref):
    total = keep_ref[...] + came_ref[...].astype(jnp.float32)
    total_ref[...] = total
    send_ref[...] = total.astype(jnp.bfloat16)


def scale_kernel(start, keep_ref, came_ref, gain_ref, after_ref, out_ref):
    rows, size = keep_ref.shape
    half = gain_ref.shape[1] // 2
    core = lax.rem(lax.axis_index("wide"), 2)
    gain = jnp.where(
        core == 0,
        gain_ref[:, start : start + size],
        gain_ref[:, half + start : half + start + size],
    )
    scaled = gain * (keep_ref[...] + came_ref[...].astype(jnp.float32))
    out_ref[:, :size] = scaled.astype(jnp.bfloat16)
    left = jnp.sum(scaled * scaled, axis=-1, keepdims=True)
    lane = lax.broadcasted_iota(jnp.int32, (rows, LANES), 1)
    tail = jnp.zeros((rows, LANES), jnp.float32)
    for piece in range(3):
        part = left.astype(jnp.bfloat16).astype(jnp.float32)
        tail = jnp.where(lane == piece, part, tail)
        left = left - part
    out_ref[:, size:] = tail.astype(jnp.bfloat16)


def chunk_scores(
    mine, start, near_ref, far_ref, wanted_ref, codes_ref, scales_ref, picks_ref, rows_ref
):
    side_rows, wide = near_ref.shape
    size = wide - LANES
    lists, list_rows, width = codes_ref.shape
    half = width // 2
    pairs = wanted_ref.shape[0]
    row = wanted_ref[:, 0:1]
    local = wanted_ref[:, 1:2]
    column = lax.broadcasted_iota(jnp.int32, (pairs, side_rows), 1)

    def pick(ref, first):
        hot = jnp.where(column + first == row, 1.0, 0.0).astype(jnp.bfloat16)
        return jnp.dot(hot, ref[...], preferred_element_type=jnp.float32)

    chosen = pick(near_ref, 0) + pick(far_ref, side_rows)
    picks_ref[...] = chosen[:, :size].astype(jnp.bfloat16)
    nothing = jnp.zeros((pairs, BLOCK), jnp.bfloat16)
    for block in range(size // BLOCK):
        span = slice(block * BLOCK, (block + 1) * BLOCK)
        kept = block % 2
        rows_ref[kept * pairs : (kept + 1) * pairs, span] = picks_ref[:, span]
        rows_ref[(1 - kept) * pairs : (2 - kept) * pairs, span] = nothing
    squares = jnp.sum(chosen[:, size:], axis=1, keepdims=True)

    core = lax.rem(lax.axis_index("wide"), 2)
    which = core if mine else 1 - core
    blocks = size // BLOCK
    here = pl.ds(
        pl.multiple_of(which * (half // BLOCK) + start // BLOCK, blocks), blocks
    )
    picked = jnp.zeros((pairs, list_rows), jnp.float32)
    for first in range(0, lists, 2):
        scale = jnp.concatenate([scales_ref[first, here, :], scales_ref[first + 1, here, :]], axis=1)
        total = jnp.zeros((pairs, 2 * list_rows), jnp.float32)
        for step in range(blocks // 2):
            span = slice(step * 2 * BLOCK, (step + 1) * 2 * BLOCK)
            away = my_span(mine, half, start + step * 2 * BLOCK, 2 * BLOCK)
            part = lax.dot_general(
                rows_ref[:, span],
                codes_ref[first : first + 2, :, away].reshape(2 * list_rows, 2 * BLOCK),
                (((1,), (1,)), ((), ())),
                preferred_element_type=jnp.float32,
            )
            total += part[:pairs] * scale[2 * step : 2 * step + 1, :]
            total += part[pairs:] * scale[2 * step + 1 : 2 * step + 2, :]
        picked = jnp.where(local == first, total[:, :list_rows], picked)
        picked = jnp.where(local == first + 1, total[:, list_rows:], picked)
    return picked, squares


def some_scores_kernel(
    mine, start, near_ref, far_ref, wanted_ref, codes_ref, scales_ref, *rest
):
    *sofar, picked_ref, squares_ref, picks_ref, rows_ref = rest
    picked, squares = chunk_scores(
        mine, start, near_ref, far_ref, wanted_ref, codes_ref, scales_ref, picks_ref, rows_ref
    )
    if sofar:
        picked += sofar[0][...]
        squares = squares + sofar[1][...]
    picked_ref[...] = picked
    squares_ref[...] = jnp.broadcast_to(squares, squares_ref.shape)


def last_scores_kernel(mine, starts, *refs):
    chunks = len(starts)
    tables = refs[2 * chunks : 2 * chunks + 3]
    sofar_ref, squares_ref, out_ref, picks_ref, rows_ref = refs[2 * chunks + 3 :]
    scores, squares = sofar_ref[...], squares_ref[:, 0:1]
    for c, start in enumerate(starts):
        picked, more = chunk_scores(
            mine, start, refs[2 * c], refs[2 * c + 1], *tables, picks_ref.at[c], rows_ref.at[c]
        )
        scores += picked
        squares = squares + more
    scores = scores * lax.rsqrt(squares + 1e-06)
    devices, capacity, _ = out_ref.shape
    for rank in range(capacity):
        out_ref[:, rank, :] = scores[rank * devices : (rank + 1) * devices]


def best_kernel(back_ref, route_ref, out_ref):
    q_dev, count = out_ref.shape
    sources, slots, list_rows = back_ref.shape
    pairs = sources * slots
    scores = back_ref[...].reshape(pairs, list_rows)
    query = route_ref[:, 0:1]
    alive = lax.broadcasted_iota(jnp.int32, (pairs, list_rows), 1) < route_ref[:, 2:3]
    left = jnp.concatenate(
        [jnp.where(alive & (query == q), scores, floor_score)[None] for q in range(q_dev)], axis=0
    )
    column = lax.broadcasted_iota(jnp.int32, (q_dev, count), 1)
    best = jnp.zeros((q_dev, count), jnp.float32)
    filled = jnp.zeros((q_dev, 1), jnp.float32)
    for rank in range(count):
        top = jnp.max(jnp.max(left, axis=1), axis=-1, keepdims=True)
        best = jnp.where(column >= filled.astype(jnp.int32), top, best)
        if rank + 1 < count:
            same = left == top[:, :, None]
            filled += jnp.sum(
                jnp.sum(jnp.where(same, 1.0, 0.0), axis=1), axis=-1, keepdims=True
            )
            left = jnp.where(same, floor_score * 2, left)
    out_ref[...] = best


def body(
    hidden_in,
    ffn_gain,
    gate_weight,
    up_weight,
    down_weight,
    final_gain,
    codes,
    scales,
    counts,
    list_slot,
    probes,
):
    q_dev, width = hidden_in.shape
    hidden_units = gate_weight.shape[1]
    n = lax.axis_size("wide")
    half = width // 2
    rows = n * q_dev
    lists_dev, list_rows, _ = codes.shape
    capacity = (q_dev * PROBES + n - 1) // n
    mib = 1 << 20
    f32, bf16 = jnp.float32, jnp.bfloat16

    def exchange(x):
        return lax.all_to_all(x, "wide", 0, 0, tiled=True)

    def swapped(x, bit):
        return lax.ppermute(x, "wide", [(i, i ^ bit) for i in range(n)])

    gate_near = pltpu.with_memory_space_constraint(gate_weight, VMEM)
    up_near = pltpu.with_memory_space_constraint(up_weight, VMEM)
    down_near = pltpu.with_memory_space_constraint(down_weight, VMEM)
    codes_near = pltpu.with_memory_space_constraint(codes, VMEM)

    normed = pl.pallas_call(
        norm_kernel,
        out_shape=shaped((q_dev, width + LANES), bf16),
        in_specs=[pl.BlockSpec(memory_space=pltpu.HBM)] * 3,
        out_specs=pl.BlockSpec(memory_space=VMEM),
        scratch_shapes=[
            VMEM((q_dev, width), bf16),
            VMEM((1, width), f32),
            VMEM(probes.shape, jnp.int32),
            pltpu.SemaphoreType.DMA((3,)),
        ],
        compiler_params=pltpu.CompilerParams(vmem_limit_bytes=8 * mib),
    )(
        pltpu.with_memory_space_constraint(hidden_in, pltpu.HBM),
        pltpu.with_memory_space_constraint(ffn_gain[None], pltpu.HBM),
        pltpu.with_memory_space_constraint(probes, pltpu.HBM),
    )
    spread = call(
        spread_kernel,
        shaped((n, q_dev, half + LANES), bf16),
        (normed,),
        8 * mib,
        cost=ahead(gate_weight, up_weight, down_weight),
    )
    here = exchange(spread)
    there = swapped(here, 1)
    gate_part, up_part = call(
        first_kernel,
        [shaped((rows, hidden_units), f32)] * 2,
        (here, gate_near, up_near, down_near),
        8 * mib,
        cost=products(rows * half * hidden_units * 2),
        scratch=[VMEM((rows, half), bf16)],
    )
    size = half // CHUNKS
    starts = [c * size for c in range(CHUNKS)]
    share = shaped((rows + 2 * q_dev, size), bf16)
    act, sent = call(
        second_kernel,
        [shaped((rows, hidden_units), bf16), share],
        (there, gate_part, up_part, gate_near, up_near, down_near, hidden_in),
        8 * mib,
        scratch=[VMEM((rows, half), bf16)],
    )
    came = [swapped(sent, 1)]
    work = products(rows * size * hidden_units)
    for start in starts[1:]:
        sent = call(
            functools.partial(share_kernel, half, start),
            share,
            (act, down_near, hidden_in),
            8 * mib,
            cost=work,
        )
        came.append(swapped(sent, 1))
    side_rows = rows // 2
    kept = [shaped((side_rows, size), f32), shaped((side_rows, size), bf16)]
    keep = []
    for c, start in enumerate(starts):
        own = call(
            functools.partial(own_kernel, half, start),
            shaped((rows, size), f32),
            (act, down_near),
            8 * mib,
            cost=work,
        )
        total, sent = call(
            functools.partial(side_kernel, start), kept, (own, came[c], hidden_in), 8 * mib
        )
        keep.append(total)
        came[c] = swapped(sent, 2)
    bit = 4
    while bit < n:
        for c in range(CHUNKS):
            keep[c], sent = call(
                sum_kernel,
                kept,
                (keep[c], came[c]),
                8 * mib,
                cost=ahead(codes) if bit == 4 and c == 0 else None,
            )
            came[c] = swapped(sent, bit)
        bit *= 2
    route = call(
        functools.partial(route_kernel, lists_dev, capacity),
        shaped((n * capacity, LANES), jnp.int32),
        (probes, list_slot[None], counts[None], keep[-1]),
        4 * mib,
    )
    wanted = call(
        functools.partial(wanted_kernel, capacity, q_dev, PROBES),
        shaped((n * capacity, LANES), jnp.int32),
        (here, list_slot[None], route),
        4 * mib,
    )
    near = [
        call(
            functools.partial(scale_kernel, start),
            shaped((side_rows, size + LANES), bf16),
            (keep[c], came[c], final_gain[None], wanted),
            8 * mib,
        )
        for c, start in enumerate(starts)
    ]
    far = []
    for x in near:
        far.append(swapped(x, 2))
    near_other = [swapped(x, 1) for x in near]
    far_other = [swapped(x, 1) for x in far]
    scales_near = jnp.swapaxes(scales, 1, 2)
    pairs = n * capacity
    sofar = []
    for c, start in enumerate(starts):
        sofar = call(
            functools.partial(some_scores_kernel, True, start),
            [shaped((pairs, list_rows), f32), shaped((pairs, LANES), f32)],
            (near[c], far[c], wanted, codes_near, scales_near, *sofar),
            8 * mib,
            cost=products(pairs * lists_dev * list_rows * size),
            scratch=[VMEM((pairs, size), bf16), VMEM((2 * pairs, size), bf16)],
        )
    others = [x for pair in zip(near_other, far_other) for x in pair]
    scores = call(
        functools.partial(last_scores_kernel, False, starts),
        shaped((n, capacity, list_rows), f32),
        (*others, wanted, codes_near, scales_near, *sofar),
        8 * mib,
        scratch=[VMEM((CHUNKS, pairs, size), bf16), VMEM((CHUNKS, 2 * pairs, size), bf16)],
    )
    back = exchange(scores)
    return call(best_kernel, shaped((q_dev, K_TOP), f32), (back, route), 8 * mib)


def solution(mesh):
    in_specs = (
        P(("grp", "wide"), None),
        P(),
        P(None, "wide"),
        P(None, "wide"),
        P("wide", None),
        P(),
        P(("grp", "wide"), None, None),
        P(("grp", "wide"), None, None),
        P("grp"),
        P("grp"),
        P(("grp", "wide"), None),
    )
    out_specs = P(("grp", "wide"), None)
    return jax.shard_map(body, mesh=mesh, in_specs=in_specs, out_specs=out_specs, check_vma=False)
```

profile of v0, /device:TPU:0, one launch (start us, length us, event | category | flops | bytes accessed | tf_op | source)
XLA Modules:
  0.0 60.1 jit_solution(2831285265812933993)
XLA Ops:
  0.0 0.9 %shard_map.109.normed_ref = bf16[4,4224]{1,0:T(4,128)(2,1)S(1)} custom-call(bf16[4,4096]{1,0:T(4,128)(2,1)} %hidden_ref.9, f32[1,4096]{1,0:T(1,128)} %bitcast.15, s32[4,8]{1,0:T(4,128)} %probes_ref.3), custom_call_target="tpu_custom_call" | custom-call | tf_op jit(solution)/shard_map/pallas_call | solution.py:414
  1.0 17.8 %all_to_all.10.here_ref = bf16[16,4,2176]{2,1,0:T(4,128)(2,1)S(1)} all-to-all(bf16[16,4,2176]{2,1,0:T(4,128)(2,1)S(1)} %shard_map.110), channel_id=1, replica_groups=mesh['grp'=2,'wide'=16] {'wide'}, dimensions={0} | all-to-all | bytes 557056 | tf_op jit(solution)/shard_map/all_to_all | solution.py:404
  18.9 1.4 %shard_map.111 = (f32[64,896]{1,0:T(8,128)S(1)}, f32[64,896]{1,0:T(8,128)S(1)}) custom-call(bf16[16,4,2176]{2,1,0:T(4,128)(2,1)S(1)} %all_to_all.10.here_ref, bf16[4096,896]{1,0:T(8,128)(2,1)S(1)} %copy-done.1, bf16[4096,896]{1,0:T(8,128)(2,1)S(1)} %copy-done.2, bf16[896,4096]{1,0:T(8,128)(2,1)S(1)} %copy-done), custom_call_target="tpu_custom_call" | custom-call | flops 469762048 | bytes 1048576 | tf_op jit(solution)/shard_map/pallas_call | solution.py:26
  20.3 1.7 %shard_map.112 = (bf16[64,896]{1,0:T(8,128)(2,1)S(1)}, bf16[72,1024]{1,0:T(8,128)(2,1)S(1)}) custom-call(bf16[16,4,2176]{2,1,0:T(4,128)(2,1)S(1)} %collective-permute-done.there_ref, f32[64,896]{1,0:T(8,128)S(1)} %get-tuple-element.25.gate_part, f32[64,896]{1,0:T(8,128)S(1)} %get-tuple-element.26.up_part, bf16[4096,896]{1,0:T(8,128)(2,1)S(1)} %copy-done.1, ...), custom_call_target="tpu_custom_call" | custom-call | tf_op jit(solution)/shard_map/pallas_call | solution.py:26
  22.0 0.5 shard_map.118
  24.0 0.5 collective-permute-start.6
  25.0 1.7 %collective-permute-start.2 = (bf16[32,1024]{1,0:T(8,128)(2,1)S(1)}, bf16[32,1024]{1,0:T(8,128)(2,1)S(1)}, u32[]{:S(2)}, u32[]{:S(2)}) collective-permute-start(bf16[32,1024]{1,0:T(8,128)(2,1)S(1)} %get-tuple-element.30), channel_id=1, source_target_pairs={{0,2},{1,3},{2,0},{3,1},{4,6},{5,7},{6,4},{7,5},{8,10},{9,11},{10,... | collective-permute-start | bytes 196616 | tf_op jit(solution)/shard_map/ppermute | solution.py:407
  26.6 2.4 %collective-permute-done.6.came_ref = bf16[32,1024]{1,0:T(8,128)(2,1)S(1)} collective-permute-done((bf16[32,1024]{1,0:T(8,128)(2,1)S(1)}, bf16[32,1024]{1,0:T(8,128)(2,1)S(1)}, u32[]{:S(2)}, u32[]{:S(2)}) %collective-permute-start.6) | collective-permute-done | bytes 65568 | tf_op jit(solution)/shard_map/ppermute | solution.py:407
  29.9 1.4 %collective-permute-start.3 = (bf16[32,1024]{1,0:T(8,128)(2,1)S(1)}, bf16[32,1024]{1,0:T(8,128)(2,1)S(1)}, u32[]{:S(2)}, u32[]{:S(2)}) collective-permute-start(bf16[32,1024]{1,0:T(8,128)(2,1)S(1)} %get-tuple-element.32), channel_id=1, source_target_pairs={{0,4},{1,5},{2,6},{3,7},{4,0},{5,1},{6,2},{7,3},{8,12},{9,13},{10,... | collective-permute-start | bytes 196616 | tf_op jit(solution)/shard_map/ppermute | solution.py:407
  31.3 2.1 %collective-permute-done.7.came_ref = bf16[32,1024]{1,0:T(8,128)(2,1)S(1)} collective-permute-done((bf16[32,1024]{1,0:T(8,128)(2,1)S(1)}, bf16[32,1024]{1,0:T(8,128)(2,1)S(1)}, u32[]{:S(2)}, u32[]{:S(2)}) %collective-permute-start.7) | collective-permute-done | bytes 65568 | tf_op jit(solution)/shard_map/ppermute | solution.py:407
  33.4 1.2 %collective-permute-start.11 = (bf16[32,1024]{1,0:T(8,128)(2,1)S(1)}, bf16[32,1024]{1,0:T(8,128)(2,1)S(1)}, u32[]{:S(2)}, u32[]{:S(2)}) collective-permute-start(bf16[32,1024]{1,0:T(8,128)(2,1)S(1)} %get-tuple-element.40), channel_id=1, source_target_pairs={{0,8},{1,9},{2,10},{3,11},{4,12},{5,13},{6,14},{7,15},{8,0},{9,1},... | collective-permute-start | bytes 196616 | tf_op jit(solution)/shard_map/ppermute | solution.py:407
  34.7 1.9 %collective-permute-start.4 = (bf16[32,1024]{1,0:T(8,128)(2,1)S(1)}, bf16[32,1024]{1,0:T(8,128)(2,1)S(1)}, u32[]{:S(2)}, u32[]{:S(2)}) collective-permute-start(bf16[32,1024]{1,0:T(8,128)(2,1)S(1)} %get-tuple-element.34), channel_id=1, source_target_pairs={{0,8},{1,9},{2,10},{3,11},{4,12},{5,13},{6,14},{7,15},{8,0},{9,1},... | collective-permute-start | bytes 196616 | tf_op jit(solution)/shard_map/ppermute | solution.py:407
  36.8 0.5 shard_map.123.after_ref.wanted_ref.refs_4_
  37.4 2.0 %collective-permute-done.11.came_ref = bf16[32,1024]{1,0:T(8,128)(2,1)S(1)} collective-permute-done((bf16[32,1024]{1,0:T(8,128)(2,1)S(1)}, bf16[32,1024]{1,0:T(8,128)(2,1)S(1)}, u32[]{:S(2)}, u32[]{:S(2)}) %collective-permute-start.11) | collective-permute-done | bytes 65568 | tf_op jit(solution)/shard_map/ppermute | solution.py:407
  39.5 0.7 %collective-permute-start.13 = (bf16[32,1152]{1,0:T(8,128)(2,1)S(1)}, bf16[32,1152]{1,0:T(8,128)(2,1)S(1)}, u32[]{:S(2)}, u32[]{:S(2)}) collective-permute-start(bf16[32,1152]{1,0:T(8,128)(2,1)S(1)} %shard_map.125.near_ref), channel_id=1, source_target_pairs={{0,2},{1,3},{2,0},{3,1},{4,6},{5,7},{6,4},{7,5},{8,10},{9,11},{10,... | collective-permute-start | bytes 221192 | tf_op jit(solution)/shard_map/ppermute | solution.py:407
  40.3 1.7 %collective-permute-start.9 = (bf16[32,1152]{1,0:T(8,128)(2,1)S(1)}, bf16[32,1152]{1,0:T(8,128)(2,1)S(1)}, u32[]{:S(2)}, u32[]{:S(2)}) collective-permute-start(bf16[32,1152]{1,0:T(8,128)(2,1)S(1)} %shard_map.124.near_ref), channel_id=1, source_target_pairs={{0,2},{1,3},{2,0},{3,1},{4,6},{5,7},{6,4},{7,5},{8,10},{9,11},{10,... | collective-permute-start | bytes 221192 | tf_op jit(solution)/shard_map/ppermute | solution.py:407
  42.0 0.5 collective-permute-start.8
  42.5 1.4 %collective-permute-done.13.far_ref = bf16[32,1152]{1,0:T(8,128)(2,1)S(1)} collective-permute-done((bf16[32,1152]{1,0:T(8,128)(2,1)S(1)}, bf16[32,1152]{1,0:T(8,128)(2,1)S(1)}, u32[]{:S(2)}, u32[]{:S(2)}) %collective-permute-start.13) | collective-permute-done | bytes 73760 | tf_op jit(solution)/shard_map/ppermute | solution.py:407
  43.9 0.8 %collective-permute-done.9.far_ref = bf16[32,1152]{1,0:T(8,128)(2,1)S(1)} collective-permute-done((bf16[32,1152]{1,0:T(8,128)(2,1)S(1)}, bf16[32,1152]{1,0:T(8,128)(2,1)S(1)}, u32[]{:S(2)}, u32[]{:S(2)}) %collective-permute-start.9) | collective-permute-done | bytes 73760 | tf_op jit(solution)/shard_map/ppermute | solution.py:407
  44.8 0.9 %shard_map.126 = (f32[32,128]{1,0:T(8,128)S(1)}, f32[32,128]{1,0:T(8,128)S(1)}) custom-call(bf16[32,1152]{1,0:T(8,128)(2,1)S(1)} %shard_map.124.near_ref, bf16[32,1152]{1,0:T(8,128)(2,1)S(1)} %collective-permute-done.9.far_ref, s32[32,128]{1,0:T(8,128)S(1)} %shard_map.123.after_ref.wanted_ref.refs_4_, bf16[8,128,4096]{2,1,0:T(8,128)(2,1)S(1)} %bitcast.6, ...), custom_call_target="tpu_custom_call" | custom-call | flops 67108864 | bytes 1048576 | tf_op jit(solution)/shard_map/pallas_call | solution.py:26
  45.7 0.9 %shard_map.127 = (f32[32,128]{1,0:T(8,128)S(1)}, f32[32,128]{1,0:T(8,128)S(1)}) custom-call(bf16[32,1152]{1,0:T(8,128)(2,1)S(1)} %shard_map.125.near_ref, bf16[32,1152]{1,0:T(8,128)(2,1)S(1)} %collective-permute-done.13.far_ref, s32[32,128]{1,0:T(8,128)S(1)} %shard_map.123.after_ref.wanted_ref.refs_4_, bf16[8,128,4096]{2,1,0:T(8,128)(2,1)S(1)} %bitcast.6, ...), custom_call_target="tpu_custom_call" | custom-call | flops 67108864 | bytes 1048576 | tf_op jit(solution)/shard_map/pallas_call | solution.py:26
  46.6 1.7 %shard_map.128 = f32[16,2,128]{2,1,0:T(2,128)S(1)} custom-call(bf16[32,1152]{1,0:T(8,128)(2,1)S(1)} %collective-permute-done.8.refs_0_, bf16[32,1152]{1,0:T(8,128)(2,1)S(1)} %collective-permute-done.10.refs_1_, bf16[32,1152]{1,0:T(8,128)(2,1)S(1)} %collective-permute-done.12.refs_2_, bf16[32,1152]{1,0:T(8,128)(2,1)S(1)} %collective-permute-done.14.refs_3_, ...), custom_call_target="tpu_custom_call" | custom-call | tf_op jit(solution)/shard_map/pallas_call | solution.py:26
  48.3 10.4 %all_to_all.11.back_ref = f32[16,2,128]{2,1,0:T(2,128)S(1)} all-to-all(f32[16,2,128]{2,1,0:T(2,128)S(1)} %shard_map.128), channel_id=1, replica_groups=mesh['grp'=2,'wide'=16] {'wide'}, dimensions={0} | all-to-all | bytes 32768 | tf_op jit(solution)/shard_map/all_to_all | solution.py:404
  58.7 1.4 %shard_map.129 = f32[4,8]{1,0:T(4,128)} custom-call(f32[16,2,128]{2,1,0:T(2,128)S(1)} %all_to_all.11.back_ref, s32[32,128]{1,0:T(8,128)S(1)} %shard_map.122.after_ref.route_ref), custom_call_target="tpu_custom_call" | custom-call | tf_op jit(solution)/shard_map/pallas_call | solution.py:26
  (52 shorter events, 3.6 us)
Async XLA Ops:
  0.9 17.9 %copy-start = (bf16[896,4096]{1,0:T(8,128)(2,1)S(1)}, bf16[896,4096]{1,0:T(8,128)(2,1)}, u32[]{:S(2)}) copy-start(bf16[896,4096]{1,0:T(8,128)(2,1)} %down_ref.7) | copy-start | bytes 22020100
  0.9 17.9 %copy-start.1 = (bf16[4096,896]{1,0:T(8,128)(2,1)S(1)}, bf16[4096,896]{1,0:T(8,128)(2,1)}, u32[]{:S(2)}) copy-start(bf16[4096,896]{1,0:T(8,128)(2,1)} %gate_ref.3) | copy-start | bytes 22020100
  1.0 17.9 %copy-start.2 = (bf16[4096,896]{1,0:T(8,128)(2,1)S(1)}, bf16[4096,896]{1,0:T(8,128)(2,1)}, u32[]{:S(2)}) copy-start(bf16[4096,896]{1,0:T(8,128)(2,1)} %up_ref.3) | copy-start | bytes 22020100
  18.8 1.6 %collective-permute-start = (bf16[16,4,2176]{2,1,0:T(4,128)(2,1)S(1)}, bf16[16,4,2176]{2,1,0:T(4,128)(2,1)S(1)}, u32[]{:S(2)}, u32[]{:S(2)}) collective-permute-start(bf16[16,4,2176]{2,1,0:T(4,128)(2,1)S(1)} %all_to_all.10.here_ref), channel_id=1, source_target_pairs={{0,1},{1,0},{2,3},{3,2},{4,5},{5,4},{6,7},{7,6},{8,9},{9,8},{10,11... | collective-permute-start | bytes 835592 | tf_op jit(solution)/shard_map/ppermute | solution.py:407
  22.5 1.4 %collective-permute-start.5 = (bf16[72,1024]{1,0:T(8,128)(2,1)S(1)}, bf16[72,1024]{1,0:T(8,128)(2,1)S(1)}, u32[]{:S(2)}, u32[]{:S(2)}) collective-permute-start(bf16[72,1024]{1,0:T(8,128)(2,1)S(1)} %shard_map.118), channel_id=1, source_target_pairs={{0,1},{1,0},{2,3},{3,2},{4,5},{5,4},{6,7},{7,6},{8,9},{9,8},{10,11... | collective-permute-start | bytes 442376 | tf_op jit(solution)/shard_map/ppermute | solution.py:407
  22.9 2.0 %collective-permute-start.1 = (bf16[72,1024]{1,0:T(8,128)(2,1)S(1)}, bf16[72,1024]{1,0:T(8,128)(2,1)S(1)}, u32[]{:S(2)}, u32[]{:S(2)}) collective-permute-start(bf16[72,1024]{1,0:T(8,128)(2,1)S(1)} %get-tuple-element.28), channel_id=1, source_target_pairs={{0,1},{1,0},{2,3},{3,2},{4,5},{5,4},{6,7},{7,6},{8,9},{9,8},{10,11... | collective-permute-start | bytes 442376 | tf_op jit(solution)/shard_map/ppermute | solution.py:407
  24.0 5.0 %collective-permute-start.6 = (bf16[32,1024]{1,0:T(8,128)(2,1)S(1)}, bf16[32,1024]{1,0:T(8,128)(2,1)S(1)}, u32[]{:S(2)}, u32[]{:S(2)}) collective-permute-start(bf16[32,1024]{1,0:T(8,128)(2,1)S(1)} %get-tuple-element.36), channel_id=1, source_target_pairs={{0,2},{1,3},{2,0},{3,1},{4,6},{5,7},{6,4},{7,5},{8,10},{9,11},{10,... | collective-permute-start | bytes 196616 | tf_op jit(solution)/shard_map/ppermute | solution.py:407
  24.5 20.2 %slice-start = ((s8[8388608]{0:T(1024)(128)(4,1)}), s8[4194304]{0:T(1024)(128)(4,1)S(1)}, s32[]{:S(2)}) async-start(s8[8388608]{0:T(1024)(128)(4,1)} %bitcast.5), calls=%async_computation.2 | async-start | bytes 8388608
  25.0 4.8 %collective-permute-start.2 = (bf16[32,1024]{1,0:T(8,128)(2,1)S(1)}, bf16[32,1024]{1,0:T(8,128)(2,1)S(1)}, u32[]{:S(2)}, u32[]{:S(2)}) collective-permute-start(bf16[32,1024]{1,0:T(8,128)(2,1)S(1)} %get-tuple-element.30), channel_id=1, source_target_pairs={{0,2},{1,3},{2,0},{3,1},{4,6},{5,7},{6,4},{7,5},{8,10},{9,11},{10,... | collective-permute-start | bytes 196616 | tf_op jit(solution)/shard_map/ppermute | solution.py:407
  29.0 4.4 %collective-permute-start.7 = (bf16[32,1024]{1,0:T(8,128)(2,1)S(1)}, bf16[32,1024]{1,0:T(8,128)(2,1)S(1)}, u32[]{:S(2)}, u32[]{:S(2)}) collective-permute-start(bf16[32,1024]{1,0:T(8,128)(2,1)S(1)} %get-tuple-element.38), channel_id=1, source_target_pairs={{0,4},{1,5},{2,6},{3,7},{4,0},{5,1},{6,2},{7,3},{8,12},{9,13},{10,... | collective-permute-start | bytes 196616 | tf_op jit(solution)/shard_map/ppermute | solution.py:407
  29.8 6.7 %copy-start.7 = (s32[128]{0:T(128)S(1)}, s32[128]{0:T(128)}, u32[]{:S(2)}) copy-start(s32[128]{0:T(128)} %param.20) | copy-start | bytes 1540
  29.8 6.7 %copy-start.8 = (s32[128]{0:T(128)S(1)}, s32[128]{0:T(128)}, u32[]{:S(2)}) copy-start(s32[128]{0:T(128)} %param.19) | copy-start | bytes 1540
  29.8 9.5 %copy-start.5 = (f32[4096]{0:T(1024)S(1)}, f32[4096]{0:T(1024)}, u32[]{:S(2)}) copy-start(f32[4096]{0:T(1024)} %param.16) | copy-start | bytes 49156
  29.8 14.9 %slice-start.1 = ((s8[8388608]{0:T(1024)(128)(4,1)}), s8[4194304]{0:T(1024)(128)(4,1)S(1)}, s32[]{:S(2)}) async-start(s8[8388608]{0:T(1024)(128)(4,1)} %bitcast.5), calls=%async_computation.3 | async-start | bytes 8388608
  29.8 14.9 %copy-start.3 = (f32[8,128,32]{1,2,0:T(8,128)S(1)}, f32[8,128,32]{1,2,0:T(8,128)}, u32[]{:S(2)}) copy-start(f32[8,128,32]{1,2,0:T(8,128)} %param.18) | copy-start | bytes 393220
  29.9 4.8 %collective-permute-start.3 = (bf16[32,1024]{1,0:T(8,128)(2,1)S(1)}, bf16[32,1024]{1,0:T(8,128)(2,1)S(1)}, u32[]{:S(2)}, u32[]{:S(2)}) collective-permute-start(bf16[32,1024]{1,0:T(8,128)(2,1)S(1)} %get-tuple-element.32), channel_id=1, source_target_pairs={{0,4},{1,5},{2,6},{3,7},{4,0},{5,1},{6,2},{7,3},{8,12},{9,13},{10,... | collective-permute-start | bytes 196616 | tf_op jit(solution)/shard_map/ppermute | solution.py:407
  33.4 5.9 %collective-permute-start.11 = (bf16[32,1024]{1,0:T(8,128)(2,1)S(1)}, bf16[32,1024]{1,0:T(8,128)(2,1)S(1)}, u32[]{:S(2)}, u32[]{:S(2)}) collective-permute-start(bf16[32,1024]{1,0:T(8,128)(2,1)S(1)} %get-tuple-element.40), channel_id=1, source_target_pairs={{0,8},{1,9},{2,10},{3,11},{4,12},{5,13},{6,14},{7,15},{8,0},{9,1},... | collective-permute-start | bytes 196616 | tf_op jit(solution)/shard_map/ppermute | solution.py:407
  34.7 5.5 %collective-permute-start.4 = (bf16[32,1024]{1,0:T(8,128)(2,1)S(1)}, bf16[32,1024]{1,0:T(8,128)(2,1)S(1)}, u32[]{:S(2)}, u32[]{:S(2)}) collective-permute-start(bf16[32,1024]{1,0:T(8,128)(2,1)S(1)} %get-tuple-element.34), channel_id=1, source_target_pairs={{0,8},{1,9},{2,10},{3,11},{4,12},{5,13},{6,14},{7,15},{8,0},{9,1},... | collective-permute-start | bytes 196616 | tf_op jit(solution)/shard_map/ppermute | solution.py:407
  39.5 4.4 %collective-permute-start.13 = (bf16[32,1152]{1,0:T(8,128)(2,1)S(1)}, bf16[32,1152]{1,0:T(8,128)(2,1)S(1)}, u32[]{:S(2)}, u32[]{:S(2)}) collective-permute-start(bf16[32,1152]{1,0:T(8,128)(2,1)S(1)} %shard_map.125.near_ref), channel_id=1, source_target_pairs={{0,2},{1,3},{2,0},{3,1},{4,6},{5,7},{6,4},{7,5},{8,10},{9,11},{10,... | collective-permute-start | bytes 221192 | tf_op jit(solution)/shard_map/ppermute | solution.py:407
  40.3 4.4 %collective-permute-start.9 = (bf16[32,1152]{1,0:T(8,128)(2,1)S(1)}, bf16[32,1152]{1,0:T(8,128)(2,1)S(1)}, u32[]{:S(2)}, u32[]{:S(2)}) collective-permute-start(bf16[32,1152]{1,0:T(8,128)(2,1)S(1)} %shard_map.124.near_ref), channel_id=1, source_target_pairs={{0,2},{1,3},{2,0},{3,1},{4,6},{5,7},{6,4},{7,5},{8,10},{9,11},{10,... | collective-permute-start | bytes 221192 | tf_op jit(solution)/shard_map/ppermute | solution.py:407
  42.0 4.6 %collective-permute-start.12 = (bf16[32,1152]{1,0:T(8,128)(2,1)S(1)}, bf16[32,1152]{1,0:T(8,128)(2,1)S(1)}, u32[]{:S(2)}, u32[]{:S(2)}) collective-permute-start(bf16[32,1152]{1,0:T(8,128)(2,1)S(1)} %shard_map.125.near_ref), channel_id=1, source_target_pairs={{0,1},{1,0},{2,3},{3,2},{4,5},{5,4},{6,7},{7,6},{8,9},{9,8},{10,11... | collective-permute-start | bytes 221192 | tf_op jit(solution)/shard_map/ppermute | solution.py:407
  42.0 4.6 %collective-permute-start.8 = (bf16[32,1152]{1,0:T(8,128)(2,1)S(1)}, bf16[32,1152]{1,0:T(8,128)(2,1)S(1)}, u32[]{:S(2)}, u32[]{:S(2)}) collective-permute-start(bf16[32,1152]{1,0:T(8,128)(2,1)S(1)} %shard_map.124.near_ref), channel_id=1, source_target_pairs={{0,1},{1,0},{2,3},{3,2},{4,5},{5,4},{6,7},{7,6},{8,9},{9,8},{10,11... | collective-permute-start | bytes 221192 | tf_op jit(solution)/shard_map/ppermute | solution.py:407
  43.9 2.7 %collective-permute-start.14 = (bf16[32,1152]{1,0:T(8,128)(2,1)S(1)}, bf16[32,1152]{1,0:T(8,128)(2,1)S(1)}, u32[]{:S(2)}, u32[]{:S(2)}) collective-permute-start(bf16[32,1152]{1,0:T(8,128)(2,1)S(1)} %collective-permute-done.13.far_ref), channel_id=1, source_target_pairs={{0,1},{1,0},{2,3},{3,2},{4,5},{5,4},{6,7},{7,6},{8,9},{9,8},{10,11... | collective-permute-start | bytes 221192 | tf_op jit(solution)/shard_map/ppermute | solution.py:407
  44.7 1.9 %collective-permute-start.10 = (bf16[32,1152]{1,0:T(8,128)(2,1)S(1)}, bf16[32,1152]{1,0:T(8,128)(2,1)S(1)}, u32[]{:S(2)}, u32[]{:S(2)}) collective-permute-start(bf16[32,1152]{1,0:T(8,128)(2,1)S(1)} %collective-permute-done.9.far_ref), channel_id=1, source_target_pairs={{0,1},{1,0},{2,3},{3,2},{4,5},{5,4},{6,7},{7,6},{8,9},{9,8},{10,11... | collective-permute-start | bytes 221192 | tf_op jit(solution)/shard_map/ppermute | solution.py:407
  (2 other events, 8.3 us)
where the time goes:
time: 60.3 us; the launch traced here: 60.1 us
  blocking collectives  28.1 us (47%)
  Pallas kernels  11.5 us (19%)
  starting transfers between devices  10.7 us (18%)
  waiting for transfers between devices  9.53 us (16%)
    all_to_all x2, blocking collectives, exchange(): return lax.all_to_all(x, 'wide', 0, 0, tiled=True)  28.1 us
    ppermute x15, starting transfers between devices, swapped(): return lax.ppermute(x, 'wide', [(i, i ^ bit) for i in range(n)])  10.7 us
    pallas_call x20, Pallas kernels, call(): pl.pallas_call(kernel, out_shape=out_shape, in_specs=[pl.BlockSpec(memory...  10.6 us
    ppermute x15, waiting for transfers between devices, swapped(): return lax.ppermute(x, 'wide', [(i, i ^ bit) for i in range(n)])  9.53 us
  transfers between devices with their start and end apart: 15, of which 8 were waited for; matrix products, arithmetic and copies ran while one was open for 0% of the time, Pallas kernels for 9%

commit v1 on v0

--- a/solution.py
+++ b/solution.py
@@ -49,22 +49,29 @@
     return jax.ShapeDtypeStruct(shape, dtype)
 
 
-def norm_kernel(hidden_ref, gain_ref, probes_ref, out_ref, rows_ref, scale_ref, ids_ref, sems):
-    copies = [
-        pltpu.make_async_copy(source, target, sems.at[index])
-        for index, (source, target) in enumerate(
-            [(hidden_ref, rows_ref), (gain_ref, scale_ref), (probes_ref, ids_ref)]
-        )
-    ]
-    for copy in copies:
-        copy.start()
-    for copy in copies:
-        copy.wait()
-    rows = rows_ref[...].astype(jnp.float32)
-    width = rows.shape[1]
+def by_core(own, other):
+    core = lax.rem(lax.axis_index("wide"), 2)
+    return jnp.where(
+        core == 0,
+        jnp.concatenate([own, other], axis=0),
+        jnp.concatenate([other, own], axis=0),
+    )
+
+
+def half_of(ref, start, size):
+    half = ref.shape[1] // 2
+    core = lax.rem(lax.axis_index("wide"), 2)
+    return jnp.where(
+        core == 0, ref[:, start : start + size], ref[:, half + start : half + start + size]
+    )
+
+
+def norm_rows(rows, gain):
     scale = lax.rsqrt(jnp.mean(rows * rows, axis=-1, keepdims=True) + 1e-05)
-    out_ref[:, :width] = (rows * scale * scale_ref[...]).astype(jnp.bfloat16)
-
+    return (rows * scale * gain).astype(jnp.bfloat16)
+
+
+def digits_of(ids_ref):
     q_dev, probes = ids_ref.shape
     pairs = q_dev * probes
     lane = lax.broadcasted_iota(jnp.int32, (q_dev, LANES), 1)
@@ -74,29 +81,73 @@
         ids = jnp.where(lane % probes == j, ids_ref[:, j : j + 1], ids)
     ids = jnp.where((lane % pairs) // probes == query, ids, 0)
     ids = jnp.sum(ids, axis=0, keepdims=True)
-    digits = jnp.where(lane < pairs, ids // DIGIT, ids % DIGIT)
-    digits = jnp.where(lane < 2 * pairs, digits, 0)
-    out_ref[:, width:] = digits.astype(jnp.float32).astype(jnp.bfloat16)
-
-
-def spread_kernel(normed_ref, out_ref):
-    half = out_ref.shape[2] - LANES
-    for k in range(out_ref.shape[0]):
-        core = k % 2
-        out_ref[k, :, :half] = normed_ref[:, core * half : (core + 1) * half]
-        out_ref[k, :, half:] = normed_ref[:, 2 * half :]
-
-
-def wanted_kernel(capacity, q_dev, probes, here_ref, slot_ref, after_ref, out_ref):
-    devices, _, wide = here_ref.shape
+    digit = jnp.where(lane < pairs, ids // DIGIT, ids % DIGIT)
+    return jnp.where(lane < 2 * pairs, digit, 0).astype(jnp.float32).astype(jnp.bfloat16)
+
+
+def norm_kernel(hidden_ref, gain_ref, probes_ref, out_ref, rows_ref, scale_ref, ids_ref, sems):
+    copies = [
+        pltpu.make_async_copy(source, target, sems.at[index])
+        for index, (source, target) in enumerate(
+            [(hidden_ref, rows_ref), (gain_ref, scale_ref), (probes_ref, ids_ref)]
+        )
+    ]
+    for copy in copies:
+        copy.start()
+    for copy in copies:
+        copy.wait()
+    width = rows_ref.shape[1]
+    out_ref[:, :width] = norm_rows(rows_ref[...].astype(jnp.float32), scale_ref[...])
+    out_ref[:, width:] = digits_of(ids_ref)
+
+
+def chip_kernel(
+    normed_ref, rows_ref, scale_ref, hidden_other, probes_other, out_ref, residual_ref
+):
+    half = out_ref.shape[1] - LANES
+    width = 2 * half
+    other = hidden_other[...].astype(jnp.float32)
+    residual_ref[...] = by_core(rows_ref[...].astype(jnp.float32), other).astype(jnp.bfloat16)
+    other = norm_rows(other, scale_ref[...]).astype(jnp.float32)
+    normed = by_core(normed_ref[:, :width].astype(jnp.float32), other)
+    core = lax.rem(lax.axis_index("wide"), 2)
+    out_ref[:, :half] = jnp.where(core == 0, normed[:, :half], normed[:, half:]).astype(
+        jnp.bfloat16
+    )
+    tails = by_core(
+        normed_ref[:, width:].astype(jnp.float32), digits_of(probes_other).astype(jnp.float32)
+    )
+    out_ref[:, half:] = tails.astype(jnp.bfloat16)
+
+
+def join_kernel(here_ref, came_ref, out_ref):
+    rows = here_ref.shape[0]
+    out_ref[:rows, :] = here_ref[...]
+    out_ref[rows:, :] = came_ref[...]
+
+
+def wanted_kernel(
+    capacity, q_dev, probes, devices, places, near_ref, far_ref, slot_ref, after_ref, out_ref
+):
+    side_rows, wide = near_ref.shape
     half = wide - LANES
     lists = slot_ref.shape[1]
     pairs = q_dev * probes
     lists_dev = lists // devices
     me = lax.axis_index("wide")
-    tails = here_ref[:, :, half:].astype(jnp.float32)
-    tails = jnp.max(tails, axis=1).astype(jnp.int32)
-    ids = tails[:, :pairs] * DIGIT + tails[:, pairs : 2 * pairs]
+    home = lax.broadcasted_iota(jnp.int32, (devices, 1), 0)
+    apart = jnp.bitwise_xor(home // 2, me // 2)
+    first = apart % 2 * side_rows + home % 2 * q_dev
+    for bit, move in places:
+        first = first + apart // (bit // 2) % 2 * move
+    column = lax.broadcasted_iota(jnp.int32, (devices, side_rows), 1)
+
+    def tails(ref, start):
+        hot = jnp.where(column + start == first, 1.0, 0.0).astype(jnp.bfloat16)
+        return jnp.dot(hot, ref[:, half:], preferred_element_type=jnp.float32)
+
+    digits = (tails(near_ref, 0) + tails(far_ref, side_rows)).astype(jnp.int32)
+    ids = digits[:, :pairs] * DIGIT + digits[:, pairs : 2 * pairs]
     number = lax.broadcasted_iota(jnp.int32, (1, lists), 1)
     local = jnp.full((devices, pairs), -1, jnp.int32)
     for index in range(lists_dev):
@@ -104,18 +155,13 @@
         mine = jnp.sum(jnp.where(held, number, 0), axis=1, keepdims=True)
         local = jnp.where(ids == mine, index, local)
     pair = lax.broadcasted_iota(jnp.int32, (devices, pairs), 1)
-    home = lax.broadcasted_iota(jnp.int32, (devices, 1), 0)
     place = lax.broadcasted_iota(jnp.int32, (devices, LANES), 1)
-    side = lax.rem(me, 4) // 2
     before = jnp.full((devices, 1), -1, jnp.int32)
     for rank in range(capacity):
         open_pair = (local >= 0) & (pair > before)
         chosen = jnp.min(jnp.where(open_pair, pair, pairs), axis=1, keepdims=True)
         there = jnp.sum(jnp.where(pair == chosen, local, 0), axis=1, keepdims=True)
-        row = jnp.where(
-            lax.rem(home, 4) // 2 == side, 0, devices * q_dev // 2
-        ) + home // 4 * (2 * q_dev) + lax.rem(home, 2) * q_dev + chosen // probes
-        row = jnp.where(chosen < pairs, row, -1)
+        row = jnp.where(chosen < pairs, first + chosen // probes, -1)
         out_ref[rank * devices : (rank + 1) * devices, :] = jnp.where(
             place == 0, row, jnp.where(place == 1, there, 0)
         )
@@ -169,29 +215,33 @@
     return pl.ds(pl.multiple_of(which * half + start, size), size)
 
 
-def first_kernel(here_ref, gate_ref, up_ref, after_ref, gate_out, up_out, rows_ref):
-    rows_ref[...] = here_ref[:, :, : rows_ref.shape[1]].reshape(rows_ref.shape)
+def fill_rows(rows_ref, near_ref, far_ref):
+    half = rows_ref.shape[1]
+    side_rows = near_ref.shape[0]
+    rows_ref[:side_rows, :] = near_ref[:, :half]
+    rows_ref[side_rows:, :] = far_ref[:, :half]
+
+
+def first_kernel(near_ref, far_ref, gate_ref, up_ref, after_ref, gate_out, up_out, rows_ref):
+    fill_rows(rows_ref, near_ref, far_ref)
     half = rows_ref.shape[1]
     span = my_span(True, half, 0, half)
     gate_out[...] = jnp.dot(rows_ref[...], gate_ref[span, :], preferred_element_type=jnp.float32)
     up_out[...] = jnp.dot(rows_ref[...], up_ref[span, :], preferred_element_type=jnp.float32)
 
 
-def put_share(act_ref, down_ref, hidden_ref, send_ref, half, start):
-    rows, size = act_ref.shape[0], send_ref.shape[1]
-    span = my_span(False, half, start, size)
-    send_ref[:rows, :] = jnp.dot(
+def share_kernel(half, start, act_ref, down_ref, send_ref):
+    span = my_span(False, half, start, send_ref.shape[1])
+    send_ref[...] = jnp.dot(
         act_ref[...], down_ref[:, span], preferred_element_type=jnp.float32
     ).astype(jnp.bfloat16)
-    residual = hidden_ref[:, span]
-    send_ref[rows:, :] = jnp.concatenate([residual, residual], axis=0)
 
 
 def second_kernel(
-    there_ref, gate_part, up_part, gate_ref, up_ref, down_ref, hidden_ref, act_ref, send_ref, rows_ref
+    near_ref, far_ref, gate_part, up_part, gate_ref, up_ref, down_ref, act_ref, send_ref, rows_ref
 ):
+    fill_rows(rows_ref, near_ref, far_ref)
     half = rows_ref.shape[1]
-    rows_ref[...] = there_ref[:, :, :half].reshape(rows_ref.shape)
     span = my_span(False, half, 0, half)
     gate = gate_part[...] + jnp.dot(
         rows_ref[...], gate_ref[span, :], preferred_element_type=jnp.float32
@@ -200,11 +250,7 @@
         rows_ref[...], up_ref[span, :], preferred_element_type=jnp.float32
     )
     act_ref[...] = (gate / (1.0 + jnp.exp(-gate)) * up).astype(jnp.bfloat16)
-    put_share(act_ref, down_ref, hidden_ref, send_ref, half, 0)
-
-
-def share_kernel(half, start, act_ref, down_ref, hidden_ref, send_ref):
-    put_share(act_ref, down_ref, hidden_ref, send_ref, half, start)
+    share_kernel(half, 0, act_ref, down_ref, send_ref)
 
 
 def own_kernel(half, start, act_ref, down_ref, own_ref):
@@ -212,52 +258,36 @@
     own_ref[...] = jnp.dot(act_ref[...], down_ref[:, span], preferred_element_type=jnp.float32)
 
 
-def side_kernel(start, own_ref, came_ref, hidden_ref, keep_ref, send_ref):
-    rows, size = own_ref.shape
-    q_dev, width = hidden_ref.shape
-    half = width // 2
-    me = lax.axis_index("wide")
-    core, side, plane = lax.rem(me, 2), lax.rem(me, 4) // 2, me // 4
-    group = 2 * q_dev
-    mine = jnp.where(
-        core == 0,
-        hidden_ref[:, start : start + size],
-        hidden_ref[:, half + start : half + start + size],
-    ).astype(jnp.float32)
-    other = came_ref[rows : rows + q_dev, :].astype(jnp.float32)
-    residual = jnp.where(
-        core == 0,
-        jnp.concatenate([mine, other], axis=0),
-        jnp.concatenate([other, mine], axis=0),
-    )
-    for z in range(rows // (2 * group)):
-        total = []
-        for y in range(2):
-            span = slice((2 * z + y) * group, (2 * z + y + 1) * group)
-            total.append(own_ref[span, :] + came_ref[span, :].astype(jnp.float32))
-        kept = jnp.where(side == 0, total[0], total[1])
-        sent = jnp.where(side == 0, total[1], total[0])
-        span = slice(z * group, (z + 1) * group)
-        keep_ref[span, :] = kept + jnp.where(plane == z, residual, jnp.zeros_like(residual))
-        send_ref[span, :] = sent.astype(jnp.bfloat16)
-
-
-def sum_kernel(keep_ref, came_ref, total_ref, send_ref):
-    total = keep_ref[...] + came_ref[...].astype(jnp.float32)
+def side_kernel(start, own_ref, came_ref, residual_ref, keep_ref, send_ref):
+    side_rows, size = keep_ref.shape
+    chip_rows = residual_ref.shape[0]
+    total = own_ref[:side_rows, :] + came_ref[:side_rows, :].astype(jnp.float32)
+    residual = half_of(residual_ref, start, size).astype(jnp.float32)
+    keep_ref[:chip_rows, :] = total[:chip_rows] + residual
+    keep_ref[chip_rows:, :] = total[chip_rows:]
+    sent = own_ref[side_rows:, :] + came_ref[side_rows:, :].astype(jnp.float32)
+    send_ref[...] = sent.astype(jnp.bfloat16)
+
+
+def met(came_ref, move):
+    rows = came_ref.shape[0]
+    blocks = [came_ref[start : start + move, :] for start in range(0, rows, move)]
+    turned = [blocks[index ^ 1] for index in range(len(blocks))]
+    return jnp.concatenate([block.astype(jnp.float32) for block in turned], axis=0)
+
+
+def sum_kernel(move, keep_ref, came_ref, total_ref, send_ref):
+    came = met(came_ref, move) if move else came_ref[...].astype(jnp.float32)
+    total = keep_ref[...] + came
     total_ref[...] = total
     send_ref[...] = total.astype(jnp.bfloat16)
 
 
-def scale_kernel(start, keep_ref, came_ref, gain_ref, after_ref, out_ref):
+def scale_kernel(start, move, keep_ref, came_ref, gain_ref, after_ref, out_ref):
     rows, size = keep_ref.shape
-    half = gain_ref.shape[1] // 2
-    core = lax.rem(lax.axis_index("wide"), 2)
-    gain = jnp.where(
-        core == 0,
-        gain_ref[:, start : start + size],
-        gain_ref[:, half + start : half + start + size],
-    )
-    scaled = gain * (keep_ref[...] + came_ref[...].astype(jnp.float32))
+    gain = half_of(gain_ref, start, size)
+    came = met(came_ref, move) if move else came_ref[...].astype(jnp.float32)
+    scaled = gain * (keep_ref[...] + came)
     out_ref[:, :size] = scaled.astype(jnp.bfloat16)
     left = jnp.sum(scaled * scaled, axis=-1, keepdims=True)
     lane = lax.broadcasted_iota(jnp.int32, (rows, LANES), 1)
@@ -411,47 +441,62 @@
     down_near = pltpu.with_memory_space_constraint(down_weight, VMEM)
     codes_near = pltpu.with_memory_space_constraint(codes, VMEM)
 
-    normed = pl.pallas_call(
+    hidden_other = swapped(hidden_in, 1)
+    probes_other = swapped(probes, 1)
+    chip_rows = 2 * q_dev
+    normed, rows_here, gain_here = pl.pallas_call(
         norm_kernel,
-        out_shape=shaped((q_dev, width + LANES), bf16),
+        out_shape=[
+            shaped((q_dev, width + LANES), bf16),
+            shaped((q_dev, width), bf16),
+            shaped((1, width), f32),
+        ],
         in_specs=[pl.BlockSpec(memory_space=pltpu.HBM)] * 3,
-        out_specs=pl.BlockSpec(memory_space=VMEM),
-        scratch_shapes=[
-            VMEM((q_dev, width), bf16),
-            VMEM((1, width), f32),
-            VMEM(probes.shape, jnp.int32),
-            pltpu.SemaphoreType.DMA((3,)),
-        ],
+        out_specs=[pl.BlockSpec(memory_space=VMEM)] * 3,
+        scratch_shapes=[VMEM(probes.shape, jnp.int32), pltpu.SemaphoreType.DMA((3,))],
         compiler_params=pltpu.CompilerParams(vmem_limit_bytes=8 * mib),
+        cost_estimate=pl.CostEstimate(flops=1 << 20, bytes_accessed=1 << 20, transcendentals=0),
     )(
         pltpu.with_memory_space_constraint(hidden_in, pltpu.HBM),
         pltpu.with_memory_space_constraint(ffn_gain[None], pltpu.HBM),
         pltpu.with_memory_space_constraint(probes, pltpu.HBM),
     )
-    spread = call(
-        spread_kernel,
-        shaped((n, q_dev, half + LANES), bf16),
-        (normed,),
+    here, residual = call(
+        chip_kernel,
+        [shaped((chip_rows, half + LANES), bf16), shaped((chip_rows, width), bf16)],
+        (normed, rows_here, gain_here, hidden_other, probes_other),
         8 * mib,
         cost=ahead(gate_weight, up_weight, down_weight),
     )
-    here = exchange(spread)
-    there = swapped(here, 1)
+    places = []
+    bit = n // 2
+    while bit > 2:
+        places.append((bit, here.shape[0]))
+        here = call(
+            join_kernel,
+            shaped((2 * here.shape[0], half + LANES), bf16),
+            (here, swapped(here, bit)),
+            4 * mib,
+        )
+        bit //= 2
+    beyond = swapped(here, 2)
+    here_other = swapped(here, 1)
+    beyond_other = swapped(beyond, 1)
     gate_part, up_part = call(
         first_kernel,
         [shaped((rows, hidden_units), f32)] * 2,
-        (here, gate_near, up_near, down_near),
+        (here, beyond, gate_near, up_near, down_near),
         8 * mib,
         cost=products(rows * half * hidden_units * 2),
         scratch=[VMEM((rows, half), bf16)],
     )
     size = half // CHUNKS
     starts = [c * size for c in range(CHUNKS)]
-    share = shaped((rows + 2 * q_dev, size), bf16)
+    share = shaped((rows, size), bf16)
     act, sent = call(
         second_kernel,
         [shaped((rows, hidden_units), bf16), share],
-        (there, gate_part, up_part, gate_near, up_near, down_near, hidden_in),
+        (here_other, beyond_other, gate_part, up_part, gate_near, up_near, down_near),
         8 * mib,
         scratch=[VMEM((rows, half), bf16)],
     )
@@ -461,7 +506,7 @@
         sent = call(
             functools.partial(share_kernel, half, start),
             share,
-            (act, down_near, hidden_in),
+            (act, down_near),
             8 * mib,
             cost=work,
         )
@@ -478,22 +523,22 @@
             cost=work,
         )
         total, sent = call(
-            functools.partial(side_kernel, start), kept, (own, came[c], hidden_in), 8 * mib
+            functools.partial(side_kernel, start), kept, (own, came[c], residual), 8 * mib
         )
         keep.append(total)
         came[c] = swapped(sent, 2)
-    bit = 4
-    while bit < n:
+    move = 0
+    for bit, next_move in reversed(places):
         for c in range(CHUNKS):
             keep[c], sent = call(
-                sum_kernel,
+                functools.partial(sum_kernel, move),
                 kept,
                 (keep[c], came[c]),
                 8 * mib,
-                cost=ahead(codes) if bit == 4 and c == 0 else None,
+                cost=ahead(codes) if move == 0 and c == 0 else None,
             )
             came[c] = swapped(sent, bit)
-        bit *= 2
+        move = next_move
     route = call(
         functools.partial(route_kernel, lists_dev, capacity),
         shaped((n * capacity, LANES), jnp.int32),
@@ -501,14 +546,14 @@
         4 * mib,
     )
     wanted = call(
-        functools.partial(wanted_kernel, capacity, q_dev, PROBES),
+        functools.partial(wanted_kernel, capacity, q_dev, PROBES, n, tuple(places)),
         shaped((n * capacity, LANES), jnp.int32),
-        (here, list_slot[None], route),
+        (here, beyond, list_slot[None], route),
         4 * mib,
     )
     near = [
         call(
-            functools.partial(scale_kernel, start),
+            functools.partial(scale_kernel, start, move),
             shaped((side_rows, size + LANES), bf16),
             (keep[c], came[c], final_gain[None], wanted),
             8 * mib,

time: 60.3 us -> 62 us (1.028)
  blocking collectives: 28.1 us -> 11.6 us
  starting transfers between devices: 10.7 us -> 23 us
  waiting for transfers between devices: 9.53 us -> 15.1 us
    all_to_all x2 -> x1, blocking collectives: 28.1 us -> 11.6 us  [exchange(): return lax.all_to_all(x, 'wide', 0, 0, tiled=True)]
    ppermute x15 -> x21, starting transfers between devices: 10.7 us -> 23 us  [swapped(): return lax.ppermute(x, 'wide', [(i, i ^ bit) for i in range(n)])]
    ppermute x15 -> x21, waiting for transfers between devices: 9.53 us -> 15.1 us  [swapped(): return lax.ppermute(x, 'wide', [(i, i ^ bit) for i in range(n)])]
    pallas_call x20 -> x22, Pallas kernels: 10.6 us -> 10.8 us  [call(): pl.pallas_call(kernel, out_shape=out_shape, in_specs=[pl.BlockSpec(memory...]
  transfers between devices with their start and end apart: 15 -> 21, of which waited for: 8 -> 11; matrix products, arithmetic and copies ran while one was open for 0% -> 0% of each run, Pallas kernels for 9% -> 10%
where the time goes in v1:
time: 62 us; the launch traced here: 61.7 us
  starting transfers between devices  23 us (37%)
  waiting for transfers between devices  15.1 us (24%)
  Pallas kernels  11.7 us (19%)
  blocking collectives  11.6 us (19%)
    ppermute x21, starting transfers between devices, swapped(): return lax.ppermute(x, 'wide', [(i, i ^ bit) for i in range(n)])  23 us
    ppermute x21, waiting for transfers between devices, swapped(): return lax.ppermute(x, 'wide', [(i, i ^ bit) for i in range(n)])  15.1 us
    all_to_all x1, blocking collectives, exchange(): return lax.all_to_all(x, 'wide', 0, 0, tiled=True)  11.6 us
    pallas_call x22, Pallas kernels, call(): pl.pallas_call(kernel, out_shape=out_shape, in_specs=[pl.BlockSpec(memory...  10.8 us
  transfers between devices with their start and end apart: 21, of which 11 were waited for; matrix products, arithmetic and copies ran while one was open for 0% of the time, Pallas kernels for 10%

profile of v1, /device:TPU:0, one launch (start us, length us, event | category | flops | bytes accessed | tf_op | source)
XLA Modules:
  0.0 61.7 jit_solution(7787968969779779046)
XLA Ops:
  0.5 0.9 %shard_map.109 = (bf16[4,4224]{1,0:T(4,128)(2,1)S(1)}, bf16[4,4096]{1,0:T(4,128)(2,1)S(1)}, f32[1,4096]{1,0:T(1,128)S(1)}) custom-call(bf16[4,4096]{1,0:T(4,128)(2,1)} %hidden_ref.1, f32[1,4096]{1,0:T(1,128)} %bitcast.15, s32[4,8]{1,0:T(4,128)} %probes_ref.3), custom_call_target="tpu_custom_call" | custom-call | flops 1048576 | bytes 1048576 | tf_op jit(solution)/shard_map/pallas_call | solution.py:447
  2.1 3.8 %collective-permute-start.2 = (bf16[8,2176]{1,0:T(8,128)(2,1)S(1)}, bf16[8,2176]{1,0:T(8,128)(2,1)S(1)}, u32[]{:S(2)}, u32[]{:S(2)}) collective-permute-start(bf16[8,2176]{1,0:T(8,128)(2,1)S(1)} %get-tuple-element.33.here_ref), channel_id=1, source_target_pairs={{0,8},{1,9},{2,10},{3,11},{4,12},{5,13},{6,14},{7,15},{8,0},{9,1},... | collective-permute-start | bytes 104456 | tf_op jit(solution)/shard_map/ppermute | solution.py:437
  5.9 1.9 %collective-permute-done.2.came_ref = bf16[8,2176]{1,0:T(8,128)(2,1)S(1)} collective-permute-done((bf16[8,2176]{1,0:T(8,128)(2,1)S(1)}, bf16[8,2176]{1,0:T(8,128)(2,1)S(1)}, u32[]{:S(2)}, u32[]{:S(2)}) %collective-permute-start.2) | collective-permute-done | bytes 34848 | tf_op jit(solution)/shard_map/ppermute | solution.py:437
  7.8 1.9 %collective-permute-start.3 = (bf16[16,2176]{1,0:T(8,128)(2,1)S(1)}, bf16[16,2176]{1,0:T(8,128)(2,1)S(1)}, u32[]{:S(2)}, u32[]{:S(2)}) collective-permute-start(bf16[16,2176]{1,0:T(8,128)(2,1)S(1)} %shard_map.111.here_ref), channel_id=1, source_target_pairs={{0,4},{1,5},{2,6},{3,7},{4,0},{5,1},{6,2},{7,3},{8,12},{9,13},{10,... | collective-permute-start | bytes 208904 | tf_op jit(solution)/shard_map/ppermute | solution.py:437
  9.7 2.4 %collective-permute-done.3.came_ref = bf16[16,2176]{1,0:T(8,128)(2,1)S(1)} collective-permute-done((bf16[16,2176]{1,0:T(8,128)(2,1)S(1)}, bf16[16,2176]{1,0:T(8,128)(2,1)S(1)}, u32[]{:S(2)}, u32[]{:S(2)}) %collective-permute-start.3) | collective-permute-done | bytes 69664 | tf_op jit(solution)/shard_map/ppermute | solution.py:437
  12.2 1.9 %collective-permute-start.5 = (bf16[32,2176]{1,0:T(8,128)(2,1)S(1)}, bf16[32,2176]{1,0:T(8,128)(2,1)S(1)}, u32[]{:S(2)}, u32[]{:S(2)}) collective-permute-start(bf16[32,2176]{1,0:T(8,128)(2,1)S(1)} %shard_map.112.near_ref), channel_id=1, source_target_pairs={{0,2},{1,3},{2,0},{3,1},{4,6},{5,7},{6,4},{7,5},{8,10},{9,11},{10,... | collective-permute-start | bytes 417800 | tf_op jit(solution)/shard_map/ppermute | solution.py:437
  14.1 3.2 %collective-permute-done.5.far_ref = bf16[32,2176]{1,0:T(8,128)(2,1)S(1)} collective-permute-done((bf16[32,2176]{1,0:T(8,128)(2,1)S(1)}, bf16[32,2176]{1,0:T(8,128)(2,1)S(1)}, u32[]{:S(2)}, u32[]{:S(2)}) %collective-permute-start.5) | collective-permute-done | bytes 139296 | tf_op jit(solution)/shard_map/ppermute | solution.py:437
  17.3 1.4 %shard_map.113 = (f32[64,896]{1,0:T(8,128)S(1)}, f32[64,896]{1,0:T(8,128)S(1)}) custom-call(bf16[32,2176]{1,0:T(8,128)(2,1)S(1)} %shard_map.112.near_ref, bf16[32,2176]{1,0:T(8,128)(2,1)S(1)} %collective-permute-done.5.far_ref, bf16[4096,896]{1,0:T(8,128)(2,1)S(1)} %copy-done.1, bf16[4096,896]{1,0:T(8,128)(2,1)S(1)} %copy-done.2, bf16[896,4096]{1,0:T(8,128)(2,1)S(1)} %copy-done), custom_call_target="tpu_custom_call" | custom-call | flops 469762048 | bytes 1048576 | tf_op jit(solution)/shard_map/pallas_call | solution.py:26
  18.7 1.7 %shard_map.114 = (bf16[64,896]{1,0:T(8,128)(2,1)S(1)}, bf16[64,1024]{1,0:T(8,128)(2,1)S(1)}) custom-call(bf16[32,2176]{1,0:T(8,128)(2,1)S(1)} %collective-permute-done.4.near_ref, bf16[32,2176]{1,0:T(8,128)(2,1)S(1)} %collective-permute-done.6.far_ref, f32[64,896]{1,0:T(8,128)S(1)} %get-tuple-element.34.gate_part, f32[64,896]{1,0:T(8,128)S(1)} %get-tuple-element.35.up_part, ...), custom_call_target="tpu_custom_call" | custom-call | tf_op jit(solution)/shard_map/pallas_call | solution.py:26
  22.5 1.9 %collective-permute-start.12 = (bf16[32,1024]{1,0:T(8,128)(2,1)S(1)}, bf16[32,1024]{1,0:T(8,128)(2,1)S(1)}, u32[]{:S(2)}, u32[]{:S(2)}) collective-permute-start(bf16[32,1024]{1,0:T(8,128)(2,1)S(1)} %get-tuple-element.46), channel_id=1, source_target_pairs={{0,2},{1,3},{2,0},{3,1},{4,6},{5,7},{6,4},{7,5},{8,10},{9,11},{10,... | collective-permute-start | bytes 196616 | tf_op jit(solution)/shard_map/ppermute | solution.py:437
  25.1 1.9 %collective-permute-done.12.came_ref = bf16[32,1024]{1,0:T(8,128)(2,1)S(1)} collective-permute-done((bf16[32,1024]{1,0:T(8,128)(2,1)S(1)}, bf16[32,1024]{1,0:T(8,128)(2,1)S(1)}, u32[]{:S(2)}, u32[]{:S(2)}) %collective-permute-start.12) | collective-permute-done | bytes 65568 | tf_op jit(solution)/shard_map/ppermute | solution.py:437
  27.0 1.9 %collective-permute-start.13 = (bf16[32,1024]{1,0:T(8,128)(2,1)S(1)}, bf16[32,1024]{1,0:T(8,128)(2,1)S(1)}, u32[]{:S(2)}, u32[]{:S(2)}) collective-permute-start(bf16[32,1024]{1,0:T(8,128)(2,1)S(1)} %get-tuple-element.48), channel_id=1, source_target_pairs={{0,4},{1,5},{2,6},{3,7},{4,0},{5,1},{6,2},{7,3},{8,12},{9,13},{10,... | collective-permute-start | bytes 196616 | tf_op jit(solution)/shard_map/ppermute | solution.py:437
  29.2 1.6 %collective-permute-start.9 = (bf16[32,1024]{1,0:T(8,128)(2,1)S(1)}, bf16[32,1024]{1,0:T(8,128)(2,1)S(1)}, u32[]{:S(2)}, u32[]{:S(2)}) collective-permute-start(bf16[32,1024]{1,0:T(8,128)(2,1)S(1)} %get-tuple-element.42), channel_id=1, source_target_pairs={{0,4},{1,5},{2,6},{3,7},{4,0},{5,1},{6,2},{7,3},{8,12},{9,13},{10,... | collective-permute-start | bytes 196616 | tf_op jit(solution)/shard_map/ppermute | solution.py:437
  30.9 0.9 %collective-permute-done.13.came_ref = bf16[32,1024]{1,0:T(8,128)(2,1)S(1)} collective-permute-done((bf16[32,1024]{1,0:T(8,128)(2,1)S(1)}, bf16[32,1024]{1,0:T(8,128)(2,1)S(1)}, u32[]{:S(2)}, u32[]{:S(2)}) %collective-permute-start.13) | collective-permute-done | bytes 65568 | tf_op jit(solution)/shard_map/ppermute | solution.py:437
  31.8 2.7 %collective-permute-start.17 = (bf16[32,1024]{1,0:T(8,128)(2,1)S(1)}, bf16[32,1024]{1,0:T(8,128)(2,1)S(1)}, u32[]{:S(2)}, u32[]{:S(2)}) collective-permute-start(bf16[32,1024]{1,0:T(8,128)(2,1)S(1)} %get-tuple-element.50), channel_id=1, source_target_pairs={{0,8},{1,9},{2,10},{3,11},{4,12},{5,13},{6,14},{7,15},{8,0},{9,1},... | collective-permute-start | bytes 196616 | tf_op jit(solution)/shard_map/ppermute | solution.py:437
  34.6 2.3 %collective-permute-start.10 = (bf16[32,1024]{1,0:T(8,128)(2,1)S(1)}, bf16[32,1024]{1,0:T(8,128)(2,1)S(1)}, u32[]{:S(2)}, u32[]{:S(2)}) collective-permute-start(bf16[32,1024]{1,0:T(8,128)(2,1)S(1)} %get-tuple-element.44), channel_id=1, source_target_pairs={{0,8},{1,9},{2,10},{3,11},{4,12},{5,13},{6,14},{7,15},{8,0},{9,1},... | collective-permute-start | bytes 196616 | tf_op jit(solution)/shard_map/ppermute | solution.py:437
  37.8 1.1 %collective-permute-done.17.came_ref = bf16[32,1024]{1,0:T(8,128)(2,1)S(1)} collective-permute-done((bf16[32,1024]{1,0:T(8,128)(2,1)S(1)}, bf16[32,1024]{1,0:T(8,128)(2,1)S(1)}, u32[]{:S(2)}, u32[]{:S(2)}) %collective-permute-start.17) | collective-permute-done | bytes 65568 | tf_op jit(solution)/shard_map/ppermute | solution.py:437
  39.0 1.6 %collective-permute-start.19 = (bf16[32,1152]{1,0:T(8,128)(2,1)S(1)}, bf16[32,1152]{1,0:T(8,128)(2,1)S(1)}, u32[]{:S(2)}, u32[]{:S(2)}) collective-permute-start(bf16[32,1152]{1,0:T(8,128)(2,1)S(1)} %shard_map.127.near_ref), channel_id=1, source_target_pairs={{0,2},{1,3},{2,0},{3,1},{4,6},{5,7},{6,4},{7,5},{8,10},{9,11},{10,... | collective-permute-start | bytes 221192 | tf_op jit(solution)/shard_map/ppermute | solution.py:437
  40.8 1.5 %collective-permute-start.15 = (bf16[32,1152]{1,0:T(8,128)(2,1)S(1)}, bf16[32,1152]{1,0:T(8,128)(2,1)S(1)}, u32[]{:S(2)}, u32[]{:S(2)}) collective-permute-start(bf16[32,1152]{1,0:T(8,128)(2,1)S(1)} %shard_map.126.near_ref), channel_id=1, source_target_pairs={{0,2},{1,3},{2,0},{3,1},{4,6},{5,7},{6,4},{7,5},{8,10},{9,11},{10,... | collective-permute-start | bytes 221192 | tf_op jit(solution)/shard_map/ppermute | solution.py:437
  43.4 1.7 %collective-permute-done.15.far_ref = bf16[32,1152]{1,0:T(8,128)(2,1)S(1)} collective-permute-done((bf16[32,1152]{1,0:T(8,128)(2,1)S(1)}, bf16[32,1152]{1,0:T(8,128)(2,1)S(1)}, u32[]{:S(2)}, u32[]{:S(2)}) %collective-permute-start.15) | collective-permute-done | bytes 73760 | tf_op jit(solution)/shard_map/ppermute | solution.py:437
  46.1 0.9 %shard_map.129 = (f32[32,128]{1,0:T(8,128)S(1)}, f32[32,128]{1,0:T(8,128)S(1)}) custom-call(bf16[32,1152]{1,0:T(8,128)(2,1)S(1)} %shard_map.127.near_ref, bf16[32,1152]{1,0:T(8,128)(2,1)S(1)} %collective-permute-done.19.far_ref, s32[32,128]{1,0:T(8,128)S(1)} %shard_map.125.after_ref.wanted_ref.refs_4_, bf16[8,128,4096]{2,1,0:T(8,128)(2,1)S(1)} %bitcast.6, ...), custom_call_target="tpu_custom_call" | custom-call | flops 67108864 | bytes 1048576 | tf_op jit(solution)/shard_map/pallas_call | solution.py:26
  47.1 1.7 %shard_map.130 = f32[16,2,128]{2,1,0:T(2,128)S(1)} custom-call(bf16[32,1152]{1,0:T(8,128)(2,1)S(1)} %collective-permute-done.14.refs_0_, bf16[32,1152]{1,0:T(8,128)(2,1)S(1)} %collective-permute-done.16.refs_1_, bf16[32,1152]{1,0:T(8,128)(2,1)S(1)} %collective-permute-done.18.refs_2_, bf16[32,1152]{1,0:T(8,128)(2,1)S(1)} %collective-permute-done.20.refs_3_, ...), custom_call_target="tpu_custom_call" | custom-call | tf_op jit(solution)/shard_map/pallas_call | solution.py:26
  48.7 11.6 %all_to_all.5.back_ref = f32[16,2,128]{2,1,0:T(2,128)S(1)} all-to-all(f32[16,2,128]{2,1,0:T(2,128)S(1)} %shard_map.130), channel_id=1, replica_groups=mesh['grp'=2,'wide'=16] {'wide'}, dimensions={0} | all-to-all | bytes 32768 | tf_op jit(solution)/shard_map/all_to_all | solution.py:434
  60.3 1.4 %shard_map.131 = f32[4,8]{1,0:T(4,128)} custom-call(f32[16,2,128]{2,1,0:T(2,128)S(1)} %all_to_all.5.back_ref, s32[32,128]{1,0:T(8,128)S(1)} %shard_map.124.after_ref.route_ref), custom_call_target="tpu_custom_call" | custom-call | tf_op jit(solution)/shard_map/pallas_call | solution.py:26
  (63 shorter events, 7.6 us)
Async XLA Ops:
  0.0 1.9 %collective-permute-start = (bf16[4,4096]{1,0:T(4,128)(2,1)}, bf16[4,4096]{1,0:T(4,128)(2,1)S(1)}, u32[]{:S(2)}, u32[]{:S(2)}) collective-permute-start(bf16[4,4096]{1,0:T(4,128)(2,1)} %hidden_ref.1), channel_id=1, source_target_pairs={{0,1},{1,0},{2,3},{3,2},{4,5},{5,4},{6,7},{7,6},{8,9},{9,8},{10,11... | collective-permute-start | bytes 98312 | tf_op jit(solution)/shard_map/ppermute | solution.py:437
  0.5 1.4 %collective-permute-start.1 = (s32[4,8]{1,0:T(4,128)}, s32[4,8]{1,0:T(4,128)S(1)}, u32[]{:S(2)}, u32[]{:S(2)}) collective-permute-start(s32[4,8]{1,0:T(4,128)} %probes_ref.3), channel_id=1, source_target_pairs={{0,1},{1,0},{2,3},{3,2},{4,5},{5,4},{6,7},{7,6},{8,9},{9,8},{10,11... | collective-permute-start | bytes 392 | tf_op jit(solution)/shard_map/ppermute | solution.py:437
  2.1 5.7 %collective-permute-start.2 = (bf16[8,2176]{1,0:T(8,128)(2,1)S(1)}, bf16[8,2176]{1,0:T(8,128)(2,1)S(1)}, u32[]{:S(2)}, u32[]{:S(2)}) collective-permute-start(bf16[8,2176]{1,0:T(8,128)(2,1)S(1)} %get-tuple-element.33.here_ref), channel_id=1, source_target_pairs={{0,8},{1,9},{2,10},{3,11},{4,12},{5,13},{6,14},{7,15},{8,0},{9,1},... | collective-permute-start | bytes 104456 | tf_op jit(solution)/shard_map/ppermute | solution.py:437
  7.8 4.3 %collective-permute-start.3 = (bf16[16,2176]{1,0:T(8,128)(2,1)S(1)}, bf16[16,2176]{1,0:T(8,128)(2,1)S(1)}, u32[]{:S(2)}, u32[]{:S(2)}) collective-permute-start(bf16[16,2176]{1,0:T(8,128)(2,1)S(1)} %shard_map.111.here_ref), channel_id=1, source_target_pairs={{0,4},{1,5},{2,6},{3,7},{4,0},{5,1},{6,2},{7,3},{8,12},{9,13},{10,... | collective-permute-start | bytes 208904 | tf_op jit(solution)/shard_map/ppermute | solution.py:437
  12.2 5.1 %collective-permute-start.5 = (bf16[32,2176]{1,0:T(8,128)(2,1)S(1)}, bf16[32,2176]{1,0:T(8,128)(2,1)S(1)}, u32[]{:S(2)}, u32[]{:S(2)}) collective-permute-start(bf16[32,2176]{1,0:T(8,128)(2,1)S(1)} %shard_map.112.near_ref), channel_id=1, source_target_pairs={{0,2},{1,3},{2,0},{3,1},{4,6},{5,7},{6,4},{7,5},{8,10},{9,11},{10,... | collective-permute-start | bytes 417800 | tf_op jit(solution)/shard_map/ppermute | solution.py:437
  14.1 4.6 %collective-permute-start.4 = (bf16[32,2176]{1,0:T(8,128)(2,1)S(1)}, bf16[32,2176]{1,0:T(8,128)(2,1)S(1)}, u32[]{:S(2)}, u32[]{:S(2)}) collective-permute-start(bf16[32,2176]{1,0:T(8,128)(2,1)S(1)} %shard_map.112.near_ref), channel_id=1, source_target_pairs={{0,1},{1,0},{2,3},{3,2},{4,5},{5,4},{6,7},{7,6},{8,9},{9,8},{10,11... | collective-permute-start | bytes 417800 | tf_op jit(solution)/shard_map/ppermute | solution.py:437
  17.3 1.4 %collective-permute-start.6 = (bf16[32,2176]{1,0:T(8,128)(2,1)S(1)}, bf16[32,2176]{1,0:T(8,128)(2,1)S(1)}, u32[]{:S(2)}, u32[]{:S(2)}) collective-permute-start(bf16[32,2176]{1,0:T(8,128)(2,1)S(1)} %collective-permute-done.5.far_ref), channel_id=1, source_target_pairs={{0,1},{1,0},{2,3},{3,2},{4,5},{5,4},{6,7},{7,6},{8,9},{9,8},{10,11... | collective-permute-start | bytes 417800 | tf_op jit(solution)/shard_map/ppermute | solution.py:437
  20.9 1.5 %collective-permute-start.11 = (bf16[64,1024]{1,0:T(8,128)(2,1)S(1)}, bf16[64,1024]{1,0:T(8,128)(2,1)S(1)}, u32[]{:S(2)}, u32[]{:S(2)}) collective-permute-start(bf16[64,1024]{1,0:T(8,128)(2,1)S(1)} %shard_map.120), channel_id=1, source_target_pairs={{0,1},{1,0},{2,3},{3,2},{4,5},{5,4},{6,7},{7,6},{8,9},{9,8},{10,11... | collective-permute-start | bytes 393224 | tf_op jit(solution)/shard_map/ppermute | solution.py:437
  21.4 3.4 %collective-permute-start.7 = (bf16[64,1024]{1,0:T(8,128)(2,1)S(1)}, bf16[64,1024]{1,0:T(8,128)(2,1)S(1)}, u32[]{:S(2)}, u32[]{:S(2)}) collective-permute-start(bf16[64,1024]{1,0:T(8,128)(2,1)S(1)} %get-tuple-element.37), channel_id=1, source_target_pairs={{0,1},{1,0},{2,3},{3,2},{4,5},{5,4},{6,7},{7,6},{8,9},{9,8},{10,11... | collective-permute-start | bytes 393224 | tf_op jit(solution)/shard_map/ppermute | solution.py:437
  22.5 4.5 %collective-permute-start.12 = (bf16[32,1024]{1,0:T(8,128)(2,1)S(1)}, bf16[32,1024]{1,0:T(8,128)(2,1)S(1)}, u32[]{:S(2)}, u32[]{:S(2)}) collective-permute-start(bf16[32,1024]{1,0:T(8,128)(2,1)S(1)} %get-tuple-element.46), channel_id=1, source_target_pairs={{0,2},{1,3},{2,0},{3,1},{4,6},{5,7},{6,4},{7,5},{8,10},{9,11},{10,... | collective-permute-start | bytes 196616 | tf_op jit(solution)/shard_map/ppermute | solution.py:437
  24.4 20.8 %slice-start = ((s8[8388608]{0:T(1024)(128)(4,1)}), s8[4194304]{0:T(1024)(128)(4,1)S(1)}, s32[]{:S(2)}) async-start(s8[8388608]{0:T(1024)(128)(4,1)} %bitcast.5), calls=%async_computation.1 | async-start | bytes 8388608
  24.8 4.3 %collective-permute-start.8 = (bf16[32,1024]{1,0:T(8,128)(2,1)S(1)}, bf16[32,1024]{1,0:T(8,128)(2,1)S(1)}, u32[]{:S(2)}, u32[]{:S(2)}) collective-permute-start(bf16[32,1024]{1,0:T(8,128)(2,1)S(1)} %get-tuple-element.40), channel_id=1, source_target_pairs={{0,2},{1,3},{2,0},{3,1},{4,6},{5,7},{6,4},{7,5},{8,10},{9,11},{10,... | collective-permute-start | bytes 196616 | tf_op jit(solution)/shard_map/ppermute | solution.py:437
  27.0 4.8 %collective-permute-start.13 = (bf16[32,1024]{1,0:T(8,128)(2,1)S(1)}, bf16[32,1024]{1,0:T(8,128)(2,1)S(1)}, u32[]{:S(2)}, u32[]{:S(2)}) collective-permute-start(bf16[32,1024]{1,0:T(8,128)(2,1)S(1)} %get-tuple-element.48), channel_id=1, source_target_pairs={{0,4},{1,5},{2,6},{3,7},{4,0},{5,1},{6,2},{7,3},{8,12},{9,13},{10,... | collective-permute-start | bytes 196616 | tf_op jit(solution)/shard_map/ppermute | solution.py:437
  29.2 16.0 %slice-start.1 = ((s8[8388608]{0:T(1024)(128)(4,1)}), s8[4194304]{0:T(1024)(128)(4,1)S(1)}, s32[]{:S(2)}) async-start(s8[8388608]{0:T(1024)(128)(4,1)} %bitcast.5), calls=%async_computation.2 | async-start | bytes 8388608
  29.2 16.0 %copy-start.3 = (f32[8,128,32]{1,2,0:T(8,128)S(1)}, f32[8,128,32]{1,2,0:T(8,128)}, u32[]{:S(2)}) copy-start(f32[8,128,32]{1,2,0:T(8,128)} %param.18) | copy-start | bytes 393220
  29.2 5.3 %collective-permute-start.9 = (bf16[32,1024]{1,0:T(8,128)(2,1)S(1)}, bf16[32,1024]{1,0:T(8,128)(2,1)S(1)}, u32[]{:S(2)}, u32[]{:S(2)}) collective-permute-start(bf16[32,1024]{1,0:T(8,128)(2,1)S(1)} %get-tuple-element.42), channel_id=1, source_target_pairs={{0,4},{1,5},{2,6},{3,7},{4,0},{5,1},{6,2},{7,3},{8,12},{9,13},{10,... | collective-permute-start | bytes 196616 | tf_op jit(solution)/shard_map/ppermute | solution.py:437
  31.8 7.1 %collective-permute-start.17 = (bf16[32,1024]{1,0:T(8,128)(2,1)S(1)}, bf16[32,1024]{1,0:T(8,128)(2,1)S(1)}, u32[]{:S(2)}, u32[]{:S(2)}) collective-permute-start(bf16[32,1024]{1,0:T(8,128)(2,1)S(1)} %get-tuple-element.50), channel_id=1, source_target_pairs={{0,8},{1,9},{2,10},{3,11},{4,12},{5,13},{6,14},{7,15},{8,0},{9,1},... | collective-permute-start | bytes 196616 | tf_op jit(solution)/shard_map/ppermute | solution.py:437
  34.6 6.0 %collective-permute-start.10 = (bf16[32,1024]{1,0:T(8,128)(2,1)S(1)}, bf16[32,1024]{1,0:T(8,128)(2,1)S(1)}, u32[]{:S(2)}, u32[]{:S(2)}) collective-permute-start(bf16[32,1024]{1,0:T(8,128)(2,1)S(1)} %get-tuple-element.44), channel_id=1, source_target_pairs={{0,8},{1,9},{2,10},{3,11},{4,12},{5,13},{6,14},{7,15},{8,0},{9,1},... | collective-permute-start | bytes 196616 | tf_op jit(solution)/shard_map/ppermute | solution.py:437
  39.0 4.4 %collective-permute-start.19 = (bf16[32,1152]{1,0:T(8,128)(2,1)S(1)}, bf16[32,1152]{1,0:T(8,128)(2,1)S(1)}, u32[]{:S(2)}, u32[]{:S(2)}) collective-permute-start(bf16[32,1152]{1,0:T(8,128)(2,1)S(1)} %shard_map.127.near_ref), channel_id=1, source_target_pairs={{0,2},{1,3},{2,0},{3,1},{4,6},{5,7},{6,4},{7,5},{8,10},{9,11},{10,... | collective-permute-start | bytes 221192 | tf_op jit(solution)/shard_map/ppermute | solution.py:437
  40.8 4.4 %collective-permute-start.15 = (bf16[32,1152]{1,0:T(8,128)(2,1)S(1)}, bf16[32,1152]{1,0:T(8,128)(2,1)S(1)}, u32[]{:S(2)}, u32[]{:S(2)}) collective-permute-start(bf16[32,1152]{1,0:T(8,128)(2,1)S(1)} %shard_map.126.near_ref), channel_id=1, source_target_pairs={{0,2},{1,3},{2,0},{3,1},{4,6},{5,7},{6,4},{7,5},{8,10},{9,11},{10,... | collective-permute-start | bytes 221192 | tf_op jit(solution)/shard_map/ppermute | solution.py:437
  42.2 4.8 %collective-permute-start.18 = (bf16[32,1152]{1,0:T(8,128)(2,1)S(1)}, bf16[32,1152]{1,0:T(8,128)(2,1)S(1)}, u32[]{:S(2)}, u32[]{:S(2)}) collective-permute-start(bf16[32,1152]{1,0:T(8,128)(2,1)S(1)} %shard_map.127.near_ref), channel_id=1, source_target_pairs={{0,1},{1,0},{2,3},{3,2},{4,5},{5,4},{6,7},{7,6},{8,9},{9,8},{10,11... | collective-permute-start | bytes 221192 | tf_op jit(solution)/shard_map/ppermute | solution.py:437
  42.2 4.8 %collective-permute-start.14 = (bf16[32,1152]{1,0:T(8,128)(2,1)S(1)}, bf16[32,1152]{1,0:T(8,128)(2,1)S(1)}, u32[]{:S(2)}, u32[]{:S(2)}) collective-permute-start(bf16[32,1152]{1,0:T(8,128)(2,1)S(1)} %shard_map.126.near_ref), channel_id=1, source_target_pairs={{0,1},{1,0},{2,3},{3,2},{4,5},{5,4},{6,7},{7,6},{8,9},{9,8},{10,11... | collective-permute-start | bytes 221192 | tf_op jit(solution)/shard_map/ppermute | solution.py:437
  43.4 3.6 %collective-permute-start.20 = (bf16[32,1152]{1,0:T(8,128)(2,1)S(1)}, bf16[32,1152]{1,0:T(8,128)(2,1)S(1)}, u32[]{:S(2)}, u32[]{:S(2)}) collective-permute-start(bf16[32,1152]{1,0:T(8,128)(2,1)S(1)} %collective-permute-done.19.far_ref), channel_id=1, source_target_pairs={{0,1},{1,0},{2,3},{3,2},{4,5},{5,4},{6,7},{7,6},{8,9},{9,8},{10,11... | collective-permute-start | bytes 221192 | tf_op jit(solution)/shard_map/ppermute | solution.py:437
  45.2 1.9 %collective-permute-start.16 = (bf16[32,1152]{1,0:T(8,128)(2,1)S(1)}, bf16[32,1152]{1,0:T(8,128)(2,1)S(1)}, u32[]{:S(2)}, u32[]{:S(2)}) collective-permute-start(bf16[32,1152]{1,0:T(8,128)(2,1)S(1)} %collective-permute-done.15.far_ref), channel_id=1, source_target_pairs={{0,1},{1,0},{2,3},{3,2},{4,5},{5,4},{6,7},{7,6},{8,9},{9,8},{10,11... | collective-permute-start | bytes 221192 | tf_op jit(solution)/shard_map/ppermute | solution.py:437
  (7 other events, 79.1 us)

commit v2 on v0

--- a/solution.py
+++ b/solution.py
@@ -12,6 +12,7 @@
 K_TOP = 8
 BLOCK = 128
 LANES = 128
+SUBLANES = 8
 DIGIT = 256
 CHUNKS = 2
 
@@ -352,6 +353,16 @@
         out_ref[:, rank, :] = scores[rank * devices : (rank + 1) * devices]
 
 
+def sort_merged(a):
+    step = len(a) // 2
+    while step:
+        for i in range(len(a)):
+            if i % (2 * step) < step:
+                a[i], a[i + step] = jnp.maximum(a[i], a[i + step]), jnp.minimum(a[i], a[i + step])
+        step //= 2
+    return a
+
+
 def best_kernel(back_ref, route_ref, out_ref):
     q_dev, count = out_ref.shape
     sources, slots, list_rows = back_ref.shape
@@ -359,22 +370,42 @@
     scores = back_ref[...].reshape(pairs, list_rows)
     query = route_ref[:, 0:1]
     alive = lax.broadcasted_iota(jnp.int32, (pairs, list_rows), 1) < route_ref[:, 2:3]
-    left = jnp.concatenate(
-        [jnp.where(alive & (query == q), scores, floor_score)[None] for q in range(q_dev)], axis=0
-    )
-    column = lax.broadcasted_iota(jnp.int32, (q_dev, count), 1)
-    best = jnp.zeros((q_dev, count), jnp.float32)
-    filled = jnp.zeros((q_dev, 1), jnp.float32)
+    lists = []
+    for q in range(q_dev):
+        left = jnp.where(alive & (query == q), scores, floor_score)
+        tiles = [[left[start : start + SUBLANES]] for start in range(0, pairs, SUBLANES)]
+        while len(tiles) > 1:
+            merged = [
+                sort_merged(one + two[::-1]) for one, two in zip(tiles[::2], tiles[1::2])
+            ]
+            tiles = [a[:count] for a in merged]
+        a = tiles[0]
+        shift = SUBLANES // 2
+        while shift:
+            b = [pltpu.roll(v, shift, 0) for v in a][::-1]
+            if 2 * len(a) <= count:
+                a = sort_merged(a + b)
+            else:
+                a = sort_merged([jnp.maximum(one, two) for one, two in zip(a, b)])
+            shift //= 2
+        lists.append(a)
+    place = lax.broadcasted_iota(jnp.int32, (SUBLANES, list_rows), 0)
+    a = []
     for rank in range(count):
-        top = jnp.max(jnp.max(left, axis=1), axis=-1, keepdims=True)
-        best = jnp.where(column >= filled.astype(jnp.int32), top, best)
-        if rank + 1 < count:
-            same = left == top[:, :, None]
-            filled += jnp.sum(
-                jnp.sum(jnp.where(same, 1.0, 0.0), axis=1), axis=-1, keepdims=True
-            )
-            left = jnp.where(same, floor_score * 2, left)
-    out_ref[...] = best
+        v = lists[0][rank]
+        for q in range(1, q_dev):
+            v = jnp.where(place == q, lists[q][rank], v)
+        a.append(v)
+    shift = list_rows // 2
+    while shift:
+        b = [pltpu.roll(v, shift, 1) for v in a][::-1]
+        a = sort_merged([jnp.maximum(one, two) for one, two in zip(a, b)])
+        shift //= 2
+    lane = lax.broadcasted_iota(jnp.int32, (SUBLANES, list_rows), 1)
+    out = a[0]
+    for rank in range(1, count):
+        out = jnp.where(lane == rank, a[rank], out)
+    out_ref[...] = out[:q_dev, :count]
 
 
 def body(
@@ -519,7 +550,9 @@
     for x in near:
         far.append(swapped(x, 2))
     near_other = [swapped(x, 1) for x in near]
-    far_other = [swapped(x, 1) for x in far]
+    far_other = []
+    for x in far:
+        far_other.append(swapped(x, 1))
     scales_near = jnp.swapaxes(scales, 1, 2)
     pairs = n * capacity
     sofar = []

time: 60.3 us -> 60.2 us (level)
  no operation moved by 1% of the time
where the time goes in v2:
time: 60.2 us; the launch traced here: 59.9 us
  blocking collectives  28.1 us (47%)
  Pallas kernels  11.3 us (19%)
  starting transfers between devices  10.7 us (18%)
  waiting for transfers between devices  9.53 us (16%)
    all_to_all x2, blocking collectives, exchange(): return lax.all_to_all(x, 'wide', 0, 0, tiled=True)  28.1 us
    ppermute x15, starting transfers between devices, swapped(): return lax.ppermute(x, 'wide', [(i, i ^ bit) for i in range(n)])  10.7 us
    pallas_call x20, Pallas kernels, call(): pl.pallas_call(kernel, out_shape=out_shape, in_specs=[pl.BlockSpec(memory...  10.4 us
    ppermute x15, waiting for transfers between devices, swapped(): return lax.ppermute(x, 'wide', [(i, i ^ bit) for i in range(n)])  9.53 us
  transfers between devices with their start and end apart: 15, of which 8 were waited for; matrix products, arithmetic and copies ran while one was open for 0% of the time, Pallas kernels for 9%

profile of v2, /device:TPU:0, one launch (start us, length us, event | category | flops | bytes accessed | tf_op | source)
XLA Modules:
  0.0 59.9 jit_solution(1079207895591147046)
XLA Ops:
  0.0 0.9 %shard_map.109.normed_ref = bf16[4,4224]{1,0:T(4,128)(2,1)S(1)} custom-call(bf16[4,4096]{1,0:T(4,128)(2,1)} %hidden_ref.9, f32[1,4096]{1,0:T(1,128)} %bitcast.15, s32[4,8]{1,0:T(4,128)} %probes_ref.3), custom_call_target="tpu_custom_call" | custom-call | tf_op jit(solution)/shard_map/pallas_call | solution.py:445
  1.0 17.8 %all_to_all.10.here_ref = bf16[16,4,2176]{2,1,0:T(4,128)(2,1)S(1)} all-to-all(bf16[16,4,2176]{2,1,0:T(4,128)(2,1)S(1)} %shard_map.110), channel_id=1, replica_groups=mesh['grp'=2,'wide'=16] {'wide'}, dimensions={0} | all-to-all | bytes 557056 | tf_op jit(solution)/shard_map/all_to_all | solution.py:435
  18.9 1.4 %shard_map.111 = (f32[64,896]{1,0:T(8,128)S(1)}, f32[64,896]{1,0:T(8,128)S(1)}) custom-call(bf16[16,4,2176]{2,1,0:T(4,128)(2,1)S(1)} %all_to_all.10.here_ref, bf16[4096,896]{1,0:T(8,128)(2,1)S(1)} %copy-done.1, bf16[4096,896]{1,0:T(8,128)(2,1)S(1)} %copy-done.2, bf16[896,4096]{1,0:T(8,128)(2,1)S(1)} %copy-done), custom_call_target="tpu_custom_call" | custom-call | flops 469762048 | bytes 1048576 | tf_op jit(solution)/shard_map/pallas_call | solution.py:27
  20.3 1.7 %shard_map.112 = (bf16[64,896]{1,0:T(8,128)(2,1)S(1)}, bf16[72,1024]{1,0:T(8,128)(2,1)S(1)}) custom-call(bf16[16,4,2176]{2,1,0:T(4,128)(2,1)S(1)} %collective-permute-done.there_ref, f32[64,896]{1,0:T(8,128)S(1)} %get-tuple-element.25.gate_part, f32[64,896]{1,0:T(8,128)S(1)} %get-tuple-element.26.up_part, bf16[4096,896]{1,0:T(8,128)(2,1)S(1)} %copy-done.1, ...), custom_call_target="tpu_custom_call" | custom-call | tf_op jit(solution)/shard_map/pallas_call | solution.py:27
  22.0 0.5 shard_map.118
  24.0 0.5 collective-permute-start.6
  25.0 1.7 %collective-permute-start.2 = (bf16[32,1024]{1,0:T(8,128)(2,1)S(1)}, bf16[32,1024]{1,0:T(8,128)(2,1)S(1)}, u32[]{:S(2)}, u32[]{:S(2)}) collective-permute-start(bf16[32,1024]{1,0:T(8,128)(2,1)S(1)} %get-tuple-element.30), channel_id=1, source_target_pairs={{0,2},{1,3},{2,0},{3,1},{4,6},{5,7},{6,4},{7,5},{8,10},{9,11},{10,... | collective-permute-start | bytes 196616 | tf_op jit(solution)/shard_map/ppermute | solution.py:438
  26.6 2.4 %collective-permute-done.6.came_ref = bf16[32,1024]{1,0:T(8,128)(2,1)S(1)} collective-permute-done((bf16[32,1024]{1,0:T(8,128)(2,1)S(1)}, bf16[32,1024]{1,0:T(8,128)(2,1)S(1)}, u32[]{:S(2)}, u32[]{:S(2)}) %collective-permute-start.6) | collective-permute-done | bytes 65568 | tf_op jit(solution)/shard_map/ppermute | solution.py:438
  29.9 1.4 %collective-permute-start.3 = (bf16[32,1024]{1,0:T(8,128)(2,1)S(1)}, bf16[32,1024]{1,0:T(8,128)(2,1)S(1)}, u32[]{:S(2)}, u32[]{:S(2)}) collective-permute-start(bf16[32,1024]{1,0:T(8,128)(2,1)S(1)} %get-tuple-element.32), channel_id=1, source_target_pairs={{0,4},{1,5},{2,6},{3,7},{4,0},{5,1},{6,2},{7,3},{8,12},{9,13},{10,... | collective-permute-start | bytes 196616 | tf_op jit(solution)/shard_map/ppermute | solution.py:438
  31.3 2.1 %collective-permute-done.7.came_ref = bf16[32,1024]{1,0:T(8,128)(2,1)S(1)} collective-permute-done((bf16[32,1024]{1,0:T(8,128)(2,1)S(1)}, bf16[32,1024]{1,0:T(8,128)(2,1)S(1)}, u32[]{:S(2)}, u32[]{:S(2)}) %collective-permute-start.7) | collective-permute-done | bytes 65568 | tf_op jit(solution)/shard_map/ppermute | solution.py:438
  33.4 1.2 %collective-permute-start.11 = (bf16[32,1024]{1,0:T(8,128)(2,1)S(1)}, bf16[32,1024]{1,0:T(8,128)(2,1)S(1)}, u32[]{:S(2)}, u32[]{:S(2)}) collective-permute-start(bf16[32,1024]{1,0:T(8,128)(2,1)S(1)} %get-tuple-element.40), channel_id=1, source_target_pairs={{0,8},{1,9},{2,10},{3,11},{4,12},{5,13},{6,14},{7,15},{8,0},{9,1},... | collective-permute-start | bytes 196616 | tf_op jit(solution)/shard_map/ppermute | solution.py:438
  34.7 1.9 %collective-permute-start.4 = (bf16[32,1024]{1,0:T(8,128)(2,1)S(1)}, bf16[32,1024]{1,0:T(8,128)(2,1)S(1)}, u32[]{:S(2)}, u32[]{:S(2)}) collective-permute-start(bf16[32,1024]{1,0:T(8,128)(2,1)S(1)} %get-tuple-element.34), channel_id=1, source_target_pairs={{0,8},{1,9},{2,10},{3,11},{4,12},{5,13},{6,14},{7,15},{8,0},{9,1},... | collective-permute-start | bytes 196616 | tf_op jit(solution)/shard_map/ppermute | solution.py:438
  36.8 0.5 shard_map.123.after_ref.wanted_ref.refs_4_
  37.4 2.0 %collective-permute-done.11.came_ref = bf16[32,1024]{1,0:T(8,128)(2,1)S(1)} collective-permute-done((bf16[32,1024]{1,0:T(8,128)(2,1)S(1)}, bf16[32,1024]{1,0:T(8,128)(2,1)S(1)}, u32[]{:S(2)}, u32[]{:S(2)}) %collective-permute-start.11) | collective-permute-done | bytes 65568 | tf_op jit(solution)/shard_map/ppermute | solution.py:438
  39.5 0.7 %collective-permute-start.13 = (bf16[32,1152]{1,0:T(8,128)(2,1)S(1)}, bf16[32,1152]{1,0:T(8,128)(2,1)S(1)}, u32[]{:S(2)}, u32[]{:S(2)}) collective-permute-start(bf16[32,1152]{1,0:T(8,128)(2,1)S(1)} %shard_map.125.near_ref), channel_id=1, source_target_pairs={{0,2},{1,3},{2,0},{3,1},{4,6},{5,7},{6,4},{7,5},{8,10},{9,11},{10,... | collective-permute-start | bytes 221192 | tf_op jit(solution)/shard_map/ppermute | solution.py:438
  40.3 1.7 %collective-permute-start.9 = (bf16[32,1152]{1,0:T(8,128)(2,1)S(1)}, bf16[32,1152]{1,0:T(8,128)(2,1)S(1)}, u32[]{:S(2)}, u32[]{:S(2)}) collective-permute-start(bf16[32,1152]{1,0:T(8,128)(2,1)S(1)} %shard_map.124.near_ref), channel_id=1, source_target_pairs={{0,2},{1,3},{2,0},{3,1},{4,6},{5,7},{6,4},{7,5},{8,10},{9,11},{10,... | collective-permute-start | bytes 221192 | tf_op jit(solution)/shard_map/ppermute | solution.py:438
  42.0 0.5 collective-permute-start.8
  42.5 1.4 %collective-permute-done.13.far_ref = bf16[32,1152]{1,0:T(8,128)(2,1)S(1)} collective-permute-done((bf16[32,1152]{1,0:T(8,128)(2,1)S(1)}, bf16[32,1152]{1,0:T(8,128)(2,1)S(1)}, u32[]{:S(2)}, u32[]{:S(2)}) %collective-permute-start.13) | collective-permute-done | bytes 73760 | tf_op jit(solution)/shard_map/ppermute | solution.py:438
  43.9 0.8 %collective-permute-done.9.far_ref = bf16[32,1152]{1,0:T(8,128)(2,1)S(1)} collective-permute-done((bf16[32,1152]{1,0:T(8,128)(2,1)S(1)}, bf16[32,1152]{1,0:T(8,128)(2,1)S(1)}, u32[]{:S(2)}, u32[]{:S(2)}) %collective-permute-start.9) | collective-permute-done | bytes 73760 | tf_op jit(solution)/shard_map/ppermute | solution.py:438
  44.8 0.9 %shard_map.126 = (f32[32,128]{1,0:T(8,128)S(1)}, f32[32,128]{1,0:T(8,128)S(1)}) custom-call(bf16[32,1152]{1,0:T(8,128)(2,1)S(1)} %shard_map.124.near_ref, bf16[32,1152]{1,0:T(8,128)(2,1)S(1)} %collective-permute-done.9.far_ref, s32[32,128]{1,0:T(8,128)S(1)} %shard_map.123.after_ref.wanted_ref.refs_4_, bf16[8,128,4096]{2,1,0:T(8,128)(2,1)S(1)} %bitcast.6, ...), custom_call_target="tpu_custom_call" | custom-call | flops 67108864 | bytes 1048576 | tf_op jit(solution)/shard_map/pallas_call | solution.py:27
  45.7 0.9 %shard_map.127 = (f32[32,128]{1,0:T(8,128)S(1)}, f32[32,128]{1,0:T(8,128)S(1)}) custom-call(bf16[32,1152]{1,0:T(8,128)(2,1)S(1)} %shard_map.125.near_ref, bf16[32,1152]{1,0:T(8,128)(2,1)S(1)} %collective-permute-done.13.far_ref, s32[32,128]{1,0:T(8,128)S(1)} %shard_map.123.after_ref.wanted_ref.refs_4_, bf16[8,128,4096]{2,1,0:T(8,128)(2,1)S(1)} %bitcast.6, ...), custom_call_target="tpu_custom_call" | custom-call | flops 67108864 | bytes 1048576 | tf_op jit(solution)/shard_map/pallas_call | solution.py:27
  46.6 1.7 %shard_map.128 = f32[16,2,128]{2,1,0:T(2,128)S(1)} custom-call(bf16[32,1152]{1,0:T(8,128)(2,1)S(1)} %collective-permute-done.8.refs_0_, bf16[32,1152]{1,0:T(8,128)(2,1)S(1)} %collective-permute-done.10.refs_1_, bf16[32,1152]{1,0:T(8,128)(2,1)S(1)} %collective-permute-done.12.refs_2_, bf16[32,1152]{1,0:T(8,128)(2,1)S(1)} %collective-permute-done.14.refs_3_, ...), custom_call_target="tpu_custom_call" | custom-call | tf_op jit(solution)/shard_map/pallas_call | solution.py:27
  48.3 10.4 %all_to_all.11.back_ref = f32[16,2,128]{2,1,0:T(2,128)S(1)} all-to-all(f32[16,2,128]{2,1,0:T(2,128)S(1)} %shard_map.128), channel_id=1, replica_groups=mesh['grp'=2,'wide'=16] {'wide'}, dimensions={0} | all-to-all | bytes 32768 | tf_op jit(solution)/shard_map/all_to_all | solution.py:435
  58.7 1.3 %shard_map.129 = f32[4,8]{1,0:T(4,128)} custom-call(f32[16,2,128]{2,1,0:T(2,128)S(1)} %all_to_all.11.back_ref, s32[32,128]{1,0:T(8,128)S(1)} %shard_map.122.after_ref.route_ref), custom_call_target="tpu_custom_call" | custom-call | tf_op jit(solution)/shard_map/pallas_call | solution.py:27
  (52 shorter events, 3.6 us)
Async XLA Ops:
  0.9 17.9 %copy-start = (bf16[896,4096]{1,0:T(8,128)(2,1)S(1)}, bf16[896,4096]{1,0:T(8,128)(2,1)}, u32[]{:S(2)}) copy-start(bf16[896,4096]{1,0:T(8,128)(2,1)} %down_ref.7) | copy-start | bytes 22020100
  0.9 17.9 %copy-start.1 = (bf16[4096,896]{1,0:T(8,128)(2,1)S(1)}, bf16[4096,896]{1,0:T(8,128)(2,1)}, u32[]{:S(2)}) copy-start(bf16[4096,896]{1,0:T(8,128)(2,1)} %gate_ref.3) | copy-start | bytes 22020100
  1.0 17.9 %copy-start.2 = (bf16[4096,896]{1,0:T(8,128)(2,1)S(1)}, bf16[4096,896]{1,0:T(8,128)(2,1)}, u32[]{:S(2)}) copy-start(bf16[4096,896]{1,0:T(8,128)(2,1)} %up_ref.3) | copy-start | bytes 22020100
  18.8 1.6 %collective-permute-start = (bf16[16,4,2176]{2,1,0:T(4,128)(2,1)S(1)}, bf16[16,4,2176]{2,1,0:T(4,128)(2,1)S(1)}, u32[]{:S(2)}, u32[]{:S(2)}) collective-permute-start(bf16[16,4,2176]{2,1,0:T(4,128)(2,1)S(1)} %all_to_all.10.here_ref), channel_id=1, source_target_pairs={{0,1},{1,0},{2,3},{3,2},{4,5},{5,4},{6,7},{7,6},{8,9},{9,8},{10,11... | collective-permute-start | bytes 835592 | tf_op jit(solution)/shard_map/ppermute | solution.py:438
  22.5 1.4 %collective-permute-start.5 = (bf16[72,1024]{1,0:T(8,128)(2,1)S(1)}, bf16[72,1024]{1,0:T(8,128)(2,1)S(1)}, u32[]{:S(2)}, u32[]{:S(2)}) collective-permute-start(bf16[72,1024]{1,0:T(8,128)(2,1)S(1)} %shard_map.118), channel_id=1, source_target_pairs={{0,1},{1,0},{2,3},{3,2},{4,5},{5,4},{6,7},{7,6},{8,9},{9,8},{10,11... | collective-permute-start | bytes 442376 | tf_op jit(solution)/shard_map/ppermute | solution.py:438
  22.9 2.0 %collective-permute-start.1 = (bf16[72,1024]{1,0:T(8,128)(2,1)S(1)}, bf16[72,1024]{1,0:T(8,128)(2,1)S(1)}, u32[]{:S(2)}, u32[]{:S(2)}) collective-permute-start(bf16[72,1024]{1,0:T(8,128)(2,1)S(1)} %get-tuple-element.28), channel_id=1, source_target_pairs={{0,1},{1,0},{2,3},{3,2},{4,5},{5,4},{6,7},{7,6},{8,9},{9,8},{10,11... | collective-permute-start | bytes 442376 | tf_op jit(solution)/shard_map/ppermute | solution.py:438
  24.0 5.0 %collective-permute-start.6 = (bf16[32,1024]{1,0:T(8,128)(2,1)S(1)}, bf16[32,1024]{1,0:T(8,128)(2,1)S(1)}, u32[]{:S(2)}, u32[]{:S(2)}) collective-permute-start(bf16[32,1024]{1,0:T(8,128)(2,1)S(1)} %get-tuple-element.36), channel_id=1, source_target_pairs={{0,2},{1,3},{2,0},{3,1},{4,6},{5,7},{6,4},{7,5},{8,10},{9,11},{10,... | collective-permute-start | bytes 196616 | tf_op jit(solution)/shard_map/ppermute | solution.py:438
  24.5 20.2 %slice-start = ((s8[8388608]{0:T(1024)(128)(4,1)}), s8[4194304]{0:T(1024)(128)(4,1)S(1)}, s32[]{:S(2)}) async-start(s8[8388608]{0:T(1024)(128)(4,1)} %bitcast.5), calls=%async_computation.2 | async-start | bytes 8388608
  25.0 4.8 %collective-permute-start.2 = (bf16[32,1024]{1,0:T(8,128)(2,1)S(1)}, bf16[32,1024]{1,0:T(8,128)(2,1)S(1)}, u32[]{:S(2)}, u32[]{:S(2)}) collective-permute-start(bf16[32,1024]{1,0:T(8,128)(2,1)S(1)} %get-tuple-element.30), channel_id=1, source_target_pairs={{0,2},{1,3},{2,0},{3,1},{4,6},{5,7},{6,4},{7,5},{8,10},{9,11},{10,... | collective-permute-start | bytes 196616 | tf_op jit(solution)/shard_map/ppermute | solution.py:438
  29.0 4.4 %collective-permute-start.7 = (bf16[32,1024]{1,0:T(8,128)(2,1)S(1)}, bf16[32,1024]{1,0:T(8,128)(2,1)S(1)}, u32[]{:S(2)}, u32[]{:S(2)}) collective-permute-start(bf16[32,1024]{1,0:T(8,128)(2,1)S(1)} %get-tuple-element.38), channel_id=1, source_target_pairs={{0,4},{1,5},{2,6},{3,7},{4,0},{5,1},{6,2},{7,3},{8,12},{9,13},{10,... | collective-permute-start | bytes 196616 | tf_op jit(solution)/shard_map/ppermute | solution.py:438
  29.8 6.7 %copy-start.7 = (s32[128]{0:T(128)S(1)}, s32[128]{0:T(128)}, u32[]{:S(2)}) copy-start(s32[128]{0:T(128)} %param.20) | copy-start | bytes 1540
  29.8 6.7 %copy-start.8 = (s32[128]{0:T(128)S(1)}, s32[128]{0:T(128)}, u32[]{:S(2)}) copy-start(s32[128]{0:T(128)} %param.19) | copy-start | bytes 1540
  29.8 9.5 %copy-start.5 = (f32[4096]{0:T(1024)S(1)}, f32[4096]{0:T(1024)}, u32[]{:S(2)}) copy-start(f32[4096]{0:T(1024)} %param.16) | copy-start | bytes 49156
  29.8 14.9 %slice-start.1 = ((s8[8388608]{0:T(1024)(128)(4,1)}), s8[4194304]{0:T(1024)(128)(4,1)S(1)}, s32[]{:S(2)}) async-start(s8[8388608]{0:T(1024)(128)(4,1)} %bitcast.5), calls=%async_computation.3 | async-start | bytes 8388608
  29.8 14.9 %copy-start.3 = (f32[8,128,32]{1,2,0:T(8,128)S(1)}, f32[8,128,32]{1,2,0:T(8,128)}, u32[]{:S(2)}) copy-start(f32[8,128,32]{1,2,0:T(8,128)} %param.18) | copy-start | bytes 393220
  29.9 4.8 %collective-permute-start.3 = (bf16[32,1024]{1,0:T(8,128)(2,1)S(1)}, bf16[32,1024]{1,0:T(8,128)(2,1)S(1)}, u32[]{:S(2)}, u32[]{:S(2)}) collective-permute-start(bf16[32,1024]{1,0:T(8,128)(2,1)S(1)} %get-tuple-element.32), channel_id=1, source_target_pairs={{0,4},{1,5},{2,6},{3,7},{4,0},{5,1},{6,2},{7,3},{8,12},{9,13},{10,... | collective-permute-start | bytes 196616 | tf_op jit(solution)/shard_map/ppermute | solution.py:438
  33.4 5.9 %collective-permute-start.11 = (bf16[32,1024]{1,0:T(8,128)(2,1)S(1)}, bf16[32,1024]{1,0:T(8,128)(2,1)S(1)}, u32[]{:S(2)}, u32[]{:S(2)}) collective-permute-start(bf16[32,1024]{1,0:T(8,128)(2,1)S(1)} %get-tuple-element.40), channel_id=1, source_target_pairs={{0,8},{1,9},{2,10},{3,11},{4,12},{5,13},{6,14},{7,15},{8,0},{9,1},... | collective-permute-start | bytes 196616 | tf_op jit(solution)/shard_map/ppermute | solution.py:438
  34.7 5.5 %collective-permute-start.4 = (bf16[32,1024]{1,0:T(8,128)(2,1)S(1)}, bf16[32,1024]{1,0:T(8,128)(2,1)S(1)}, u32[]{:S(2)}, u32[]{:S(2)}) collective-permute-start(bf16[32,1024]{1,0:T(8,128)(2,1)S(1)} %get-tuple-element.34), channel_id=1, source_target_pairs={{0,8},{1,9},{2,10},{3,11},{4,12},{5,13},{6,14},{7,15},{8,0},{9,1},... | collective-permute-start | bytes 196616 | tf_op jit(solution)/shard_map/ppermute | solution.py:438
  39.5 4.4 %collective-permute-start.13 = (bf16[32,1152]{1,0:T(8,128)(2,1)S(1)}, bf16[32,1152]{1,0:T(8,128)(2,1)S(1)}, u32[]{:S(2)}, u32[]{:S(2)}) collective-permute-start(bf16[32,1152]{1,0:T(8,128)(2,1)S(1)} %shard_map.125.near_ref), channel_id=1, source_target_pairs={{0,2},{1,3},{2,0},{3,1},{4,6},{5,7},{6,4},{7,5},{8,10},{9,11},{10,... | collective-permute-start | bytes 221192 | tf_op jit(solution)/shard_map/ppermute | solution.py:438
  40.3 4.4 %collective-permute-start.9 = (bf16[32,1152]{1,0:T(8,128)(2,1)S(1)}, bf16[32,1152]{1,0:T(8,128)(2,1)S(1)}, u32[]{:S(2)}, u32[]{:S(2)}) collective-permute-start(bf16[32,1152]{1,0:T(8,128)(2,1)S(1)} %shard_map.124.near_ref), channel_id=1, source_target_pairs={{0,2},{1,3},{2,0},{3,1},{4,6},{5,7},{6,4},{7,5},{8,10},{9,11},{10,... | collective-permute-start | bytes 221192 | tf_op jit(solution)/shard_map/ppermute | solution.py:438
  42.0 4.6 %collective-permute-start.12 = (bf16[32,1152]{1,0:T(8,128)(2,1)S(1)}, bf16[32,1152]{1,0:T(8,128)(2,1)S(1)}, u32[]{:S(2)}, u32[]{:S(2)}) collective-permute-start(bf16[32,1152]{1,0:T(8,128)(2,1)S(1)} %shard_map.125.near_ref), channel_id=1, source_target_pairs={{0,1},{1,0},{2,3},{3,2},{4,5},{5,4},{6,7},{7,6},{8,9},{9,8},{10,11... | collective-permute-start | bytes 221192 | tf_op jit(solution)/shard_map/ppermute | solution.py:438
  42.0 4.6 %collective-permute-start.8 = (bf16[32,1152]{1,0:T(8,128)(2,1)S(1)}, bf16[32,1152]{1,0:T(8,128)(2,1)S(1)}, u32[]{:S(2)}, u32[]{:S(2)}) collective-permute-start(bf16[32,1152]{1,0:T(8,128)(2,1)S(1)} %shard_map.124.near_ref), channel_id=1, source_target_pairs={{0,1},{1,0},{2,3},{3,2},{4,5},{5,4},{6,7},{7,6},{8,9},{9,8},{10,11... | collective-permute-start | bytes 221192 | tf_op jit(solution)/shard_map/ppermute | solution.py:438
  43.9 2.7 %collective-permute-start.14 = (bf16[32,1152]{1,0:T(8,128)(2,1)S(1)}, bf16[32,1152]{1,0:T(8,128)(2,1)S(1)}, u32[]{:S(2)}, u32[]{:S(2)}) collective-permute-start(bf16[32,1152]{1,0:T(8,128)(2,1)S(1)} %collective-permute-done.13.far_ref), channel_id=1, source_target_pairs={{0,1},{1,0},{2,3},{3,2},{4,5},{5,4},{6,7},{7,6},{8,9},{9,8},{10,11... | collective-permute-start | bytes 221192 | tf_op jit(solution)/shard_map/ppermute | solution.py:438
  44.7 1.9 %collective-permute-start.10 = (bf16[32,1152]{1,0:T(8,128)(2,1)S(1)}, bf16[32,1152]{1,0:T(8,128)(2,1)S(1)}, u32[]{:S(2)}, u32[]{:S(2)}) collective-permute-start(bf16[32,1152]{1,0:T(8,128)(2,1)S(1)} %collective-permute-done.9.far_ref), channel_id=1, source_target_pairs={{0,1},{1,0},{2,3},{3,2},{4,5},{5,4},{6,7},{7,6},{8,9},{9,8},{10,11... | collective-permute-start | bytes 221192 | tf_op jit(solution)/shard_map/ppermute | solution.py:438
  (2 other events, 8.3 us)

commit v3 on v2

--- a/solution.py
+++ b/solution.py
@@ -204,7 +204,7 @@
     put_share(act_ref, down_ref, hidden_ref, send_ref, half, 0)
 
 
-def share_kernel(half, start, act_ref, down_ref, hidden_ref, send_ref):
+def share_kernel(half, start, act_ref, down_ref, hidden_ref, after_ref, send_ref):
     put_share(act_ref, down_ref, hidden_ref, send_ref, half, start)
 
 
@@ -486,21 +486,20 @@
         8 * mib,
         scratch=[VMEM((rows, half), bf16)],
     )
-    came = [swapped(sent, 1)]
     work = products(rows * size * hidden_units)
-    for start in starts[1:]:
-        sent = call(
-            functools.partial(share_kernel, half, start),
-            share,
-            (act, down_near, hidden_in),
-            8 * mib,
-            cost=work,
-        )
-        came.append(swapped(sent, 1))
     side_rows = rows // 2
     kept = [shaped((side_rows, size), f32), shaped((side_rows, size), bf16)]
-    keep = []
+    keep, came = [], []
     for c, start in enumerate(starts):
+        if c:
+            sent = call(
+                functools.partial(share_kernel, half, start),
+                share,
+                (act, down_near, hidden_in, own),
+                8 * mib,
+                cost=work,
+            )
+        crossed = swapped(sent, 1)
         own = call(
             functools.partial(own_kernel, half, start),
             shaped((rows, size), f32),
@@ -509,10 +508,10 @@
             cost=work,
         )
         total, sent = call(
-            functools.partial(side_kernel, start), kept, (own, came[c], hidden_in), 8 * mib
+            functools.partial(side_kernel, start), kept, (own, crossed, hidden_in), 8 * mib
         )
         keep.append(total)
-        came[c] = swapped(sent, 2)
+        came.append(swapped(sent, 2))
     bit = 4
     while bit < n:
         for c in range(CHUNKS):
@@ -549,7 +548,9 @@
     far = []
     for x in near:
         far.append(swapped(x, 2))
-    near_other = [swapped(x, 1) for x in near]
+    near_other = []
+    for x in near:
+        near_other.append(swapped(x, 1))
     far_other = []
     for x in far:
         far_other.append(swapped(x, 1))

time: 60.2 us -> 60.6 us (level)
  waiting for transfers between devices: 9.53 us -> 10.3 us
    ppermute x15, waiting for transfers between devices: 9.53 us -> 10.3 us  [swapped(): return lax.ppermute(x, 'wide', [(i, i ^ bit) for i in range(n)])]
  transfers between devices with their start and end apart: 15 -> 15, of which waited for: 8 -> 9; matrix products, arithmetic and copies ran while one was open for 0% -> 0% of each run, Pallas kernels for 9% -> 8%
where the time goes in v3:
time: 60.6 us; the launch traced here: 60.4 us
  blocking collectives  28.2 us (47%)
  Pallas kernels  11.4 us (19%)
  waiting for transfers between devices  10.3 us (17%)
  starting transfers between devices  10.2 us (17%)
    all_to_all x2, blocking collectives, exchange(): return lax.all_to_all(x, 'wide', 0, 0, tiled=True)  28.2 us
    pallas_call x20, Pallas kernels, call(): pl.pallas_call(kernel, out_shape=out_shape, in_specs=[pl.BlockSpec(memory...  10.4 us
    ppermute x15, waiting for transfers between devices, swapped(): return lax.ppermute(x, 'wide', [(i, i ^ bit) for i in range(n)])  10.3 us
    ppermute x15, starting transfers between devices, swapped(): return lax.ppermute(x, 'wide', [(i, i ^ bit) for i in range(n)])  10.2 us
  transfers between devices with their start and end apart: 15, of which 9 were waited for; matrix products, arithmetic and copies ran while one was open for 0% of the time, Pallas kernels for 8%

profile of v3, /device:TPU:0, one launch (start us, length us, event | category | flops | bytes accessed | tf_op | source)
XLA Modules:
  0.0 60.4 jit_solution(5442014700902523778)
XLA Ops:
  0.0 0.9 %shard_map.109.normed_ref = bf16[4,4224]{1,0:T(4,128)(2,1)S(1)} custom-call(bf16[4,4096]{1,0:T(4,128)(2,1)} %hidden_ref.9, f32[1,4096]{1,0:T(1,128)} %bitcast.15, s32[4,8]{1,0:T(4,128)} %probes_ref.3), custom_call_target="tpu_custom_call" | custom-call | tf_op jit(solution)/shard_map/pallas_call | solution.py:445
  1.0 17.8 %all_to_all.10.here_ref = bf16[16,4,2176]{2,1,0:T(4,128)(2,1)S(1)} all-to-all(bf16[16,4,2176]{2,1,0:T(4,128)(2,1)S(1)} %shard_map.110), channel_id=1, replica_groups=mesh['grp'=2,'wide'=16] {'wide'}, dimensions={0} | all-to-all | bytes 557056 | tf_op jit(solution)/shard_map/all_to_all | solution.py:435
  18.9 1.4 %shard_map.111 = (f32[64,896]{1,0:T(8,128)S(1)}, f32[64,896]{1,0:T(8,128)S(1)}) custom-call(bf16[16,4,2176]{2,1,0:T(4,128)(2,1)S(1)} %all_to_all.10.here_ref, bf16[4096,896]{1,0:T(8,128)(2,1)S(1)} %copy-done.1, bf16[4096,896]{1,0:T(8,128)(2,1)S(1)} %copy-done.2, bf16[896,4096]{1,0:T(8,128)(2,1)S(1)} %copy-done), custom_call_target="tpu_custom_call" | custom-call | flops 469762048 | bytes 1048576 | tf_op jit(solution)/shard_map/pallas_call | solution.py:27
  20.3 1.7 %shard_map.112 = (bf16[64,896]{1,0:T(8,128)(2,1)S(1)}, bf16[72,1024]{1,0:T(8,128)(2,1)S(1)}) custom-call(bf16[16,4,2176]{2,1,0:T(4,128)(2,1)S(1)} %collective-permute-done.there_ref, f32[64,896]{1,0:T(8,128)S(1)} %get-tuple-element.25.gate_part, f32[64,896]{1,0:T(8,128)S(1)} %get-tuple-element.26.up_part, bf16[4096,896]{1,0:T(8,128)(2,1)S(1)} %copy-done.1, ...), custom_call_target="tpu_custom_call" | custom-call | tf_op jit(solution)/shard_map/pallas_call | solution.py:27
  22.5 0.5 shard_map.118
  24.4 0.5 collective-permute-start.6
  25.0 1.7 %collective-permute-start.2 = (bf16[32,1024]{1,0:T(8,128)(2,1)S(1)}, bf16[32,1024]{1,0:T(8,128)(2,1)S(1)}, u32[]{:S(2)}, u32[]{:S(2)}) collective-permute-start(bf16[32,1024]{1,0:T(8,128)(2,1)S(1)} %get-tuple-element.30), channel_id=1, source_target_pairs={{0,2},{1,3},{2,0},{3,1},{4,6},{5,7},{6,4},{7,5},{8,10},{9,11},{10,... | collective-permute-start | bytes 196616 | tf_op jit(solution)/shard_map/ppermute | solution.py:438
  26.6 2.8 %collective-permute-done.6.came_ref = bf16[32,1024]{1,0:T(8,128)(2,1)S(1)} collective-permute-done((bf16[32,1024]{1,0:T(8,128)(2,1)S(1)}, bf16[32,1024]{1,0:T(8,128)(2,1)S(1)}, u32[]{:S(2)}, u32[]{:S(2)}) %collective-permute-start.6) | collective-permute-done | bytes 65568 | tf_op jit(solution)/shard_map/ppermute | solution.py:438
  29.5 0.6 collective-permute-start.7
  30.3 1.4 %collective-permute-start.3 = (bf16[32,1024]{1,0:T(8,128)(2,1)S(1)}, bf16[32,1024]{1,0:T(8,128)(2,1)S(1)}, u32[]{:S(2)}, u32[]{:S(2)}) collective-permute-start(bf16[32,1024]{1,0:T(8,128)(2,1)S(1)} %get-tuple-element.32), channel_id=1, source_target_pairs={{0,4},{1,5},{2,6},{3,7},{4,0},{5,1},{6,2},{7,3},{8,12},{9,13},{10,... | collective-permute-start | bytes 196616 | tf_op jit(solution)/shard_map/ppermute | solution.py:438
  31.7 2.1 %collective-permute-done.7.came_ref = bf16[32,1024]{1,0:T(8,128)(2,1)S(1)} collective-permute-done((bf16[32,1024]{1,0:T(8,128)(2,1)S(1)}, bf16[32,1024]{1,0:T(8,128)(2,1)S(1)}, u32[]{:S(2)}, u32[]{:S(2)}) %collective-permute-start.7) | collective-permute-done | bytes 65568 | tf_op jit(solution)/shard_map/ppermute | solution.py:438
  33.9 1.2 %collective-permute-start.11 = (bf16[32,1024]{1,0:T(8,128)(2,1)S(1)}, bf16[32,1024]{1,0:T(8,128)(2,1)S(1)}, u32[]{:S(2)}, u32[]{:S(2)}) collective-permute-start(bf16[32,1024]{1,0:T(8,128)(2,1)S(1)} %get-tuple-element.40), channel_id=1, source_target_pairs={{0,8},{1,9},{2,10},{3,11},{4,12},{5,13},{6,14},{7,15},{8,0},{9,1},... | collective-permute-start | bytes 196616 | tf_op jit(solution)/shard_map/ppermute | solution.py:438
  35.1 1.9 %collective-permute-start.4 = (bf16[32,1024]{1,0:T(8,128)(2,1)S(1)}, bf16[32,1024]{1,0:T(8,128)(2,1)S(1)}, u32[]{:S(2)}, u32[]{:S(2)}) collective-permute-start(bf16[32,1024]{1,0:T(8,128)(2,1)S(1)} %get-tuple-element.34), channel_id=1, source_target_pairs={{0,8},{1,9},{2,10},{3,11},{4,12},{5,13},{6,14},{7,15},{8,0},{9,1},... | collective-permute-start | bytes 196616 | tf_op jit(solution)/shard_map/ppermute | solution.py:438
  37.3 0.5 shard_map.123.after_ref.wanted_ref.refs_4_
  37.8 1.9 %collective-permute-done.11.came_ref = bf16[32,1024]{1,0:T(8,128)(2,1)S(1)} collective-permute-done((bf16[32,1024]{1,0:T(8,128)(2,1)S(1)}, bf16[32,1024]{1,0:T(8,128)(2,1)S(1)}, u32[]{:S(2)}, u32[]{:S(2)}) %collective-permute-start.11) | collective-permute-done | bytes 65568 | tf_op jit(solution)/shard_map/ppermute | solution.py:438
  40.5 1.6 %collective-permute-start.9 = (bf16[32,1152]{1,0:T(8,128)(2,1)S(1)}, bf16[32,1152]{1,0:T(8,128)(2,1)S(1)}, u32[]{:S(2)}, u32[]{:S(2)}) collective-permute-start(bf16[32,1152]{1,0:T(8,128)(2,1)S(1)} %shard_map.124.near_ref), channel_id=1, source_target_pairs={{0,2},{1,3},{2,0},{3,1},{4,6},{5,7},{6,4},{7,5},{8,10},{9,11},{10,... | collective-permute-start | bytes 221192 | tf_op jit(solution)/shard_map/ppermute | solution.py:438
  42.1 0.5 collective-permute-start.8
  42.6 1.6 %collective-permute-done.13.far_ref = bf16[32,1152]{1,0:T(8,128)(2,1)S(1)} collective-permute-done((bf16[32,1152]{1,0:T(8,128)(2,1)S(1)}, bf16[32,1152]{1,0:T(8,128)(2,1)S(1)}, u32[]{:S(2)}, u32[]{:S(2)}) %collective-permute-start.13) | collective-permute-done | bytes 73760 | tf_op jit(solution)/shard_map/ppermute | solution.py:438
  44.3 0.8 %collective-permute-done.9.far_ref = bf16[32,1152]{1,0:T(8,128)(2,1)S(1)} collective-permute-done((bf16[32,1152]{1,0:T(8,128)(2,1)S(1)}, bf16[32,1152]{1,0:T(8,128)(2,1)S(1)}, u32[]{:S(2)}, u32[]{:S(2)}) %collective-permute-start.9) | collective-permute-done | bytes 73760 | tf_op jit(solution)/shard_map/ppermute | solution.py:438
  45.1 0.9 %shard_map.126 = (f32[32,128]{1,0:T(8,128)S(1)}, f32[32,128]{1,0:T(8,128)S(1)}) custom-call(bf16[32,1152]{1,0:T(8,128)(2,1)S(1)} %shard_map.124.near_ref, bf16[32,1152]{1,0:T(8,128)(2,1)S(1)} %collective-permute-done.9.far_ref, s32[32,128]{1,0:T(8,128)S(1)} %shard_map.123.after_ref.wanted_ref.refs_4_, bf16[8,128,4096]{2,1,0:T(8,128)(2,1)S(1)} %bitcast.6, ...), custom_call_target="tpu_custom_call" | custom-call | flops 67108864 | bytes 1048576 | tf_op jit(solution)/shard_map/pallas_call | solution.py:27
  46.0 0.9 %shard_map.127 = (f32[32,128]{1,0:T(8,128)S(1)}, f32[32,128]{1,0:T(8,128)S(1)}) custom-call(bf16[32,1152]{1,0:T(8,128)(2,1)S(1)} %shard_map.125.near_ref, bf16[32,1152]{1,0:T(8,128)(2,1)S(1)} %collective-permute-done.13.far_ref, s32[32,128]{1,0:T(8,128)S(1)} %shard_map.123.after_ref.wanted_ref.refs_4_, bf16[8,128,4096]{2,1,0:T(8,128)(2,1)S(1)} %bitcast.6, ...), custom_call_target="tpu_custom_call" | custom-call | flops 67108864 | bytes 1048576 | tf_op jit(solution)/shard_map/pallas_call | solution.py:27
  46.9 1.7 %shard_map.128 = f32[16,2,128]{2,1,0:T(2,128)S(1)} custom-call(bf16[32,1152]{1,0:T(8,128)(2,1)S(1)} %collective-permute-done.8.refs_0_, bf16[32,1152]{1,0:T(8,128)(2,1)S(1)} %collective-permute-done.10.refs_1_, bf16[32,1152]{1,0:T(8,128)(2,1)S(1)} %collective-permute-done.12.refs_2_, bf16[32,1152]{1,0:T(8,128)(2,1)S(1)} %collective-permute-done.14.refs_3_, ...), custom_call_target="tpu_custom_call" | custom-call | tf_op jit(solution)/shard_map/pallas_call | solution.py:27
  48.6 10.5 %all_to_all.11.back_ref = f32[16,2,128]{2,1,0:T(2,128)S(1)} all-to-all(f32[16,2,128]{2,1,0:T(2,128)S(1)} %shard_map.128), channel_id=1, replica_groups=mesh['grp'=2,'wide'=16] {'wide'}, dimensions={0} | all-to-all | bytes 32768 | tf_op jit(solution)/shard_map/all_to_all | solution.py:435
  59.1 1.3 %shard_map.129 = f32[4,8]{1,0:T(4,128)} custom-call(f32[16,2,128]{2,1,0:T(2,128)S(1)} %all_to_all.11.back_ref, s32[32,128]{1,0:T(8,128)S(1)} %shard_map.122.after_ref.route_ref), custom_call_target="tpu_custom_call" | custom-call | tf_op jit(solution)/shard_map/pallas_call | solution.py:27
  (52 shorter events, 3.6 us)
Async XLA Ops:
  0.9 17.9 %copy-start = (bf16[896,4096]{1,0:T(8,128)(2,1)S(1)}, bf16[896,4096]{1,0:T(8,128)(2,1)}, u32[]{:S(2)}) copy-start(bf16[896,4096]{1,0:T(8,128)(2,1)} %down_ref.7) | copy-start | bytes 22020100
  0.9 17.9 %copy-start.1 = (bf16[4096,896]{1,0:T(8,128)(2,1)S(1)}, bf16[4096,896]{1,0:T(8,128)(2,1)}, u32[]{:S(2)}) copy-start(bf16[4096,896]{1,0:T(8,128)(2,1)} %gate_ref.3) | copy-start | bytes 22020100
  1.0 17.9 %copy-start.2 = (bf16[4096,896]{1,0:T(8,128)(2,1)S(1)}, bf16[4096,896]{1,0:T(8,128)(2,1)}, u32[]{:S(2)}) copy-start(bf16[4096,896]{1,0:T(8,128)(2,1)} %up_ref.3) | copy-start | bytes 22020100
  18.8 1.6 %collective-permute-start = (bf16[16,4,2176]{2,1,0:T(4,128)(2,1)S(1)}, bf16[16,4,2176]{2,1,0:T(4,128)(2,1)S(1)}, u32[]{:S(2)}, u32[]{:S(2)}) collective-permute-start(bf16[16,4,2176]{2,1,0:T(4,128)(2,1)S(1)} %all_to_all.10.here_ref), channel_id=1, source_target_pairs={{0,1},{1,0},{2,3},{3,2},{4,5},{5,4},{6,7},{7,6},{8,9},{9,8},{10,11... | collective-permute-start | bytes 835592 | tf_op jit(solution)/shard_map/ppermute | solution.py:438
  22.9 1.4 %collective-permute-start.5 = (bf16[72,1024]{1,0:T(8,128)(2,1)S(1)}, bf16[72,1024]{1,0:T(8,128)(2,1)S(1)}, u32[]{:S(2)}, u32[]{:S(2)}) collective-permute-start(bf16[72,1024]{1,0:T(8,128)(2,1)S(1)} %shard_map.118), channel_id=1, source_target_pairs={{0,1},{1,0},{2,3},{3,2},{4,5},{5,4},{6,7},{7,6},{8,9},{9,8},{10,11... | collective-permute-start | bytes 442376 | tf_op jit(solution)/shard_map/ppermute | solution.py:438
  23.4 1.6 %collective-permute-start.1 = (bf16[72,1024]{1,0:T(8,128)(2,1)S(1)}, bf16[72,1024]{1,0:T(8,128)(2,1)S(1)}, u32[]{:S(2)}, u32[]{:S(2)}) collective-permute-start(bf16[72,1024]{1,0:T(8,128)(2,1)S(1)} %get-tuple-element.28), channel_id=1, source_target_pairs={{0,1},{1,0},{2,3},{3,2},{4,5},{5,4},{6,7},{7,6},{8,9},{9,8},{10,11... | collective-permute-start | bytes 442376 | tf_op jit(solution)/shard_map/ppermute | solution.py:438
  23.5 21.5 %slice-start = ((s8[8388608]{0:T(1024)(128)(4,1)}), s8[4194304]{0:T(1024)(128)(4,1)S(1)}, s32[]{:S(2)}) async-start(s8[8388608]{0:T(1024)(128)(4,1)} %bitcast.5), calls=%async_computation.2 | async-start | bytes 8388608
  24.4 5.0 %collective-permute-start.6 = (bf16[32,1024]{1,0:T(8,128)(2,1)S(1)}, bf16[32,1024]{1,0:T(8,128)(2,1)S(1)}, u32[]{:S(2)}, u32[]{:S(2)}) collective-permute-start(bf16[32,1024]{1,0:T(8,128)(2,1)S(1)} %get-tuple-element.36), channel_id=1, source_target_pairs={{0,2},{1,3},{2,0},{3,1},{4,6},{5,7},{6,4},{7,5},{8,10},{9,11},{10,... | collective-permute-start | bytes 196616 | tf_op jit(solution)/shard_map/ppermute | solution.py:438
  25.0 5.3 %collective-permute-start.2 = (bf16[32,1024]{1,0:T(8,128)(2,1)S(1)}, bf16[32,1024]{1,0:T(8,128)(2,1)S(1)}, u32[]{:S(2)}, u32[]{:S(2)}) collective-permute-start(bf16[32,1024]{1,0:T(8,128)(2,1)S(1)} %get-tuple-element.30), channel_id=1, source_target_pairs={{0,2},{1,3},{2,0},{3,1},{4,6},{5,7},{6,4},{7,5},{8,10},{9,11},{10,... | collective-permute-start | bytes 196616 | tf_op jit(solution)/shard_map/ppermute | solution.py:438
  29.5 4.4 %collective-permute-start.7 = (bf16[32,1024]{1,0:T(8,128)(2,1)S(1)}, bf16[32,1024]{1,0:T(8,128)(2,1)S(1)}, u32[]{:S(2)}, u32[]{:S(2)}) collective-permute-start(bf16[32,1024]{1,0:T(8,128)(2,1)S(1)} %get-tuple-element.38), channel_id=1, source_target_pairs={{0,4},{1,5},{2,6},{3,7},{4,0},{5,1},{6,2},{7,3},{8,12},{9,13},{10,... | collective-permute-start | bytes 196616 | tf_op jit(solution)/shard_map/ppermute | solution.py:438
  30.3 6.7 %copy-start.7 = (s32[128]{0:T(128)S(1)}, s32[128]{0:T(128)}, u32[]{:S(2)}) copy-start(s32[128]{0:T(128)} %param.20) | copy-start | bytes 1540
  30.3 6.7 %copy-start.8 = (s32[128]{0:T(128)S(1)}, s32[128]{0:T(128)}, u32[]{:S(2)}) copy-start(s32[128]{0:T(128)} %param.19) | copy-start | bytes 1540
  30.3 9.5 %copy-start.5 = (f32[4096]{0:T(1024)S(1)}, f32[4096]{0:T(1024)}, u32[]{:S(2)}) copy-start(f32[4096]{0:T(1024)} %param.16) | copy-start | bytes 49156
  30.3 14.8 %slice-start.1 = ((s8[8388608]{0:T(1024)(128)(4,1)}), s8[4194304]{0:T(1024)(128)(4,1)S(1)}, s32[]{:S(2)}) async-start(s8[8388608]{0:T(1024)(128)(4,1)} %bitcast.5), calls=%async_computation.3 | async-start | bytes 8388608
  30.3 14.8 %copy-start.3 = (f32[8,128,32]{1,2,0:T(8,128)S(1)}, f32[8,128,32]{1,2,0:T(8,128)}, u32[]{:S(2)}) copy-start(f32[8,128,32]{1,2,0:T(8,128)} %param.18) | copy-start | bytes 393220
  30.3 4.8 %collective-permute-start.3 = (bf16[32,1024]{1,0:T(8,128)(2,1)S(1)}, bf16[32,1024]{1,0:T(8,128)(2,1)S(1)}, u32[]{:S(2)}, u32[]{:S(2)}) collective-permute-start(bf16[32,1024]{1,0:T(8,128)(2,1)S(1)} %get-tuple-element.32), channel_id=1, source_target_pairs={{0,4},{1,5},{2,6},{3,7},{4,0},{5,1},{6,2},{7,3},{8,12},{9,13},{10,... | collective-permute-start | bytes 196616 | tf_op jit(solution)/shard_map/ppermute | solution.py:438
  33.9 5.8 %collective-permute-start.11 = (bf16[32,1024]{1,0:T(8,128)(2,1)S(1)}, bf16[32,1024]{1,0:T(8,128)(2,1)S(1)}, u32[]{:S(2)}, u32[]{:S(2)}) collective-permute-start(bf16[32,1024]{1,0:T(8,128)(2,1)S(1)} %get-tuple-element.40), channel_id=1, source_target_pairs={{0,8},{1,9},{2,10},{3,11},{4,12},{5,13},{6,14},{7,15},{8,0},{9,1},... | collective-permute-start | bytes 196616 | tf_op jit(solution)/shard_map/ppermute | solution.py:438
  35.1 5.3 %collective-permute-start.4 = (bf16[32,1024]{1,0:T(8,128)(2,1)S(1)}, bf16[32,1024]{1,0:T(8,128)(2,1)S(1)}, u32[]{:S(2)}, u32[]{:S(2)}) collective-permute-start(bf16[32,1024]{1,0:T(8,128)(2,1)S(1)} %get-tuple-element.34), channel_id=1, source_target_pairs={{0,8},{1,9},{2,10},{3,11},{4,12},{5,13},{6,14},{7,15},{8,0},{9,1},... | collective-permute-start | bytes 196616 | tf_op jit(solution)/shard_map/ppermute | solution.py:438
  39.8 4.4 %collective-permute-start.13 = (bf16[32,1152]{1,0:T(8,128)(2,1)S(1)}, bf16[32,1152]{1,0:T(8,128)(2,1)S(1)}, u32[]{:S(2)}, u32[]{:S(2)}) collective-permute-start(bf16[32,1152]{1,0:T(8,128)(2,1)S(1)} %shard_map.125.near_ref), channel_id=1, source_target_pairs={{0,2},{1,3},{2,0},{3,1},{4,6},{5,7},{6,4},{7,5},{8,10},{9,11},{10,... | collective-permute-start | bytes 221192 | tf_op jit(solution)/shard_map/ppermute | solution.py:438
  40.5 4.5 %collective-permute-start.9 = (bf16[32,1152]{1,0:T(8,128)(2,1)S(1)}, bf16[32,1152]{1,0:T(8,128)(2,1)S(1)}, u32[]{:S(2)}, u32[]{:S(2)}) collective-permute-start(bf16[32,1152]{1,0:T(8,128)(2,1)S(1)} %shard_map.124.near_ref), channel_id=1, source_target_pairs={{0,2},{1,3},{2,0},{3,1},{4,6},{5,7},{6,4},{7,5},{8,10},{9,11},{10,... | collective-permute-start | bytes 221192 | tf_op jit(solution)/shard_map/ppermute | solution.py:438
  42.1 4.8 %collective-permute-start.12 = (bf16[32,1152]{1,0:T(8,128)(2,1)S(1)}, bf16[32,1152]{1,0:T(8,128)(2,1)S(1)}, u32[]{:S(2)}, u32[]{:S(2)}) collective-permute-start(bf16[32,1152]{1,0:T(8,128)(2,1)S(1)} %shard_map.125.near_ref), channel_id=1, source_target_pairs={{0,1},{1,0},{2,3},{3,2},{4,5},{5,4},{6,7},{7,6},{8,9},{9,8},{10,11... | collective-permute-start | bytes 221192 | tf_op jit(solution)/shard_map/ppermute | solution.py:438
  42.1 4.8 %collective-permute-start.8 = (bf16[32,1152]{1,0:T(8,128)(2,1)S(1)}, bf16[32,1152]{1,0:T(8,128)(2,1)S(1)}, u32[]{:S(2)}, u32[]{:S(2)}) collective-permute-start(bf16[32,1152]{1,0:T(8,128)(2,1)S(1)} %shard_map.124.near_ref), channel_id=1, source_target_pairs={{0,1},{1,0},{2,3},{3,2},{4,5},{5,4},{6,7},{7,6},{8,9},{9,8},{10,11... | collective-permute-start | bytes 221192 | tf_op jit(solution)/shard_map/ppermute | solution.py:438
  44.3 2.7 %collective-permute-start.14 = (bf16[32,1152]{1,0:T(8,128)(2,1)S(1)}, bf16[32,1152]{1,0:T(8,128)(2,1)S(1)}, u32[]{:S(2)}, u32[]{:S(2)}) collective-permute-start(bf16[32,1152]{1,0:T(8,128)(2,1)S(1)} %collective-permute-done.13.far_ref), channel_id=1, source_target_pairs={{0,1},{1,0},{2,3},{3,2},{4,5},{5,4},{6,7},{7,6},{8,9},{9,8},{10,11... | collective-permute-start | bytes 221192 | tf_op jit(solution)/shard_map/ppermute | solution.py:438
  45.1 1.9 %collective-permute-start.10 = (bf16[32,1152]{1,0:T(8,128)(2,1)S(1)}, bf16[32,1152]{1,0:T(8,128)(2,1)S(1)}, u32[]{:S(2)}, u32[]{:S(2)}) collective-permute-start(bf16[32,1152]{1,0:T(8,128)(2,1)S(1)} %collective-permute-done.9.far_ref), channel_id=1, source_target_pairs={{0,1},{1,0},{2,3},{3,2},{4,5},{5,4},{6,7},{7,6},{8,9},{9,8},{10,11... | collective-permute-start | bytes 221192 | tf_op jit(solution)/shard_map/ppermute | solution.py:438
  (2 other events, 8.3 us)
